TPU v7x, 32 devices: a whole 2x2x4 slice. The times are simulated.
32 devices in a mesh: pb: 8 (over y, x, core), pa: 4 (over z).
Axes of the slice: x: 2, y: 2, z: 4, core: 2. Of those that a mesh axis runs over, the one named last changes fastest.
Arguments:
- query_states: bfloat16 [2048, 768], P(('pb', 'pa')), may hold values from -6 to 6
- passage_states: bfloat16 [24576, 768], P(('pb', 'pa')), may hold values from -6 to 6
- passage_bins: int32 [32, 768], P(('pb', 'pa')), may hold values from 0 to 3, never falling along the last dimension, each value on 1 to 512 neighbouring positions
- padding_mask: int32 [32, 768], P(('pb', 'pa')), may hold values 0 or 1
- token_ids: int32 [32, 768], P(('pb', 'pa')), may hold values from 0 to 30521
- positives: int32 [64], replicated, may hold values from 0 to 127
- united_weight: bfloat16 [768, 2304], replicated, may hold values from -0.21875 to 0.21875
- output_weight: bfloat16 [768, 768], replicated, may hold values from -0.875 to 0.875
- first_gain: float32 [768], replicated, may hold values from 0.1 to 1.9
- first_shift: float32 [768], replicated, may hold values from -3 to 3
- up_weight: bfloat16 [768, 3072], replicated, may hold values from -0.21875 to 0.21875
- up_bias: float32 [3072], replicated, may hold values from -3 to 3
- down_weight: bfloat16 [3072, 768], replicated, may hold values from -0.109375 to 0.109375
- second_gain: float32 [768], replicated, may hold values from 0.1 to 1.9
- second_shift: float32 [768], replicated, may hold values from -3 to 3
- project_weight: bfloat16 [768, 128], replicated, may hold values from -0.21875 to 0.21875
Outputs:
- query_embeddings: bfloat16 [2048, 128], P(('pb', 'pa'))
- passage_embeddings: bfloat16 [24576, 128], P(('pb', 'pa'))
- query_losses: float32 [64], P(('pb', 'pa'))
- grad_query_states: float32 [2048, 768], P(('pb', 'pa'))
- grad_passage_states: float32 [24576, 768], P(('pb', 'pa'))
- grad_united: float32 [768, 2304], P(('pb', 'pa'))
- grad_output: float32 [768, 768], P(('pb', 'pa'))
- grad_first_gain: float32 [768], P(('pb', 'pa'))
- grad_first_shift: float32 [768], P(('pb', 'pa'))
- grad_up: float32 [768, 3072], P(('pb', 'pa'))
- grad_up_bias: float32 [3072], P(('pb', 'pa'))
- grad_down: float32 [3072, 768], P(('pb', 'pa'))
- grad_second_gain: float32 [768], P(('pb', 'pa'))
- grad_second_shift: float32 [768], P(('pb', 'pa'))
- grad_project: float32 [768, 128], P(('pb', 'pa'))
Inputs may be any that keep to these rules, and one draw needn't show every extreme that they name: `passage_bins`: within each row of 768 tokens the bin numbers never fall, every bin holds 1 to 512 tokens, and one bin holds exactly 512.
All inputs are finite; a program needn't handle non-finite values. No bound on the sum of `padding_mask` on one device may be relied on, other than what follows from the above.
Results may differ from a plain program's by a relative error of at most 0.014.
Values may be sent and summed in bfloat16 or wider, within the bound.
No kernel may reach another device: no remote copies, remote signals or barrier semaphores. Data moves between devices by JAX's collectives and lax.ppermute only.
A program may use at most 320 MiB of HBM per device.

v0:
```python
import jax
import jax.numpy as jnp
from jax import lax
from jax.sharding import PartitionSpec as P

D = 768
HEAD_DIM = 64
HEADS = 12
PROJ = 128
QLEN = 32
QRY_DEV = 2
PSG_DEV = 4
SKIP_IDS = 3000


SOFT_TEMP = 0.1
LOGIT_GAIN = 8.0
NORM_EPSILON = 1e-06
MASK_FILL = -1000000000.0
SCORE_SCALE = 0.125


def merged_2(part, axis, combine):
    gathered = jax.tree.map(lambda a: lax.all_gather(a, axis), part)

    def take(source):
        return jax.tree.map(lambda a: lax.dynamic_index_in_dim(a, source, 0, False), gathered)

    return lax.fori_loop(
        1, lax.axis_size(axis), lambda source, state: combine(state, take(source)), take(0)
    )


def layer_norm(hidden, gain_row, shift_row):
    centred = hidden - jnp.mean(hidden, axis=-1, keepdims=True)
    spread = jnp.mean(centred * centred, axis=-1, keepdims=True)
    return centred * lax.rsqrt(spread + NORM_EPSILON) * gain_row + shift_row


def unit_rows(projected):
    return projected * lax.rsqrt(
        jnp.sum(projected * projected, axis=-1, keepdims=True) + NORM_EPSILON
    )


def exact_gelu(inputs):
    return jax.nn.gelu(inputs, approximate=False)


def contract_rows(operand, partner):
    return jnp.einsum("rd,re->de", operand, partner, preferred_element_type=jnp.float32)


def times_transposed(operand, partner):
    return jnp.einsum("re,de->rd", operand, partner, preferred_element_type=jnp.float32)


def split_heads(united_rows):
    stacked = united_rows.reshape(united_rows.shape[0], 3, HEADS, HEAD_DIM)
    return (stacked[:, 0], stacked[:, 1], stacked[:, 2])


def head_scores(head_query, head_key, allowed):
    raw_scores = (
        jnp.einsum("qhd,khd->hqk", head_query, head_key, preferred_element_type=jnp.float32)
        * SCORE_SCALE
    )
    return jnp.where(allowed[None], raw_scores, MASK_FILL)


def attend_forward(united_rows, allowed):
    head_query, head_key, head_value = split_heads(united_rows)
    scores = head_scores(head_query, head_key, allowed)
    row_peak = jnp.max(scores, axis=-1, keepdims=True)
    log_total = jnp.log(jnp.sum(jnp.exp(scores - row_peak), axis=-1, keepdims=True)) + row_peak
    weights = jnp.exp(scores - log_total).astype(jnp.bfloat16)
    attended = jnp.einsum("hqk,khd->qhd", weights, head_value, preferred_element_type=jnp.float32)
    return (attended.reshape(united_rows.shape[0], D).astype(jnp.bfloat16), log_total)


def attend_backward(united_rows, allowed, log_total, grad_attended):
    head_query, head_key, head_value = split_heads(united_rows)
    grad_heads = grad_attended.reshape(united_rows.shape[0], HEADS, HEAD_DIM)
    soft_weights = jnp.exp(head_scores(head_query, head_key, allowed) - log_total)
    weights_low = soft_weights.astype(jnp.bfloat16)
    grad_weights = jnp.einsum(
        "qhd,khd->hqk", grad_heads, head_value, preferred_element_type=jnp.float32
    )
    centre = jnp.sum(soft_weights * grad_weights, axis=-1, keepdims=True)
    grad_scores = (soft_weights * (grad_weights - centre)).astype(jnp.bfloat16)
    grad_query = (
        jnp.einsum("hqk,khd->qhd", grad_scores, head_key, preferred_element_type=jnp.float32)
        * SCORE_SCALE
    )
    grad_key = (
        jnp.einsum("hqk,qhd->khd", grad_scores, head_query, preferred_element_type=jnp.float32)
        * SCORE_SCALE
    )
    grad_value = jnp.einsum(
        "hqk,qhd->khd", weights_low, grad_heads, preferred_element_type=jnp.float32
    )
    joined = jnp.stack([grad_query, grad_key, grad_value], axis=1)
    return joined.reshape(united_rows.shape[0], 3 * D).astype(jnp.bfloat16)


def bin_members(codes):
    slot_ids = lax.broadcasted_iota(jnp.int32, (codes.shape[0], PSG_DEV), 1)
    return (codes[:, None] == slot_ids).astype(jnp.float32)


def tile_forward(query_part, passage_part, member):
    similarity = jnp.einsum(
        "te,pe->tp", query_part, passage_part, preferred_element_type=jnp.float32
    )
    exp_sim = jnp.exp(similarity / SOFT_TEMP)
    bin_sums = jnp.dot(exp_sim, member, precision=lax.Precision.HIGHEST)
    return (exp_sim, bin_sums)


def tile_backward(exp_sim, member, bin_sums, grad_bins, query_part, passage_part):
    weight_bins = grad_bins / (1.0 + bin_sums)
    spread = jnp.dot(weight_bins, jnp.transpose(member), precision=lax.Precision.HIGHEST)
    grad_sim = (exp_sim * spread).astype(jnp.bfloat16)
    grad_query = jnp.einsum("tp,pe->te", grad_sim, passage_part, preferred_element_type=jnp.float32)
    grad_passage = jnp.einsum("tp,te->pe", grad_sim, query_part, preferred_element_type=jnp.float32)
    return (grad_query, grad_passage)


def query_logits(bin_sums):
    terms = SOFT_TEMP * jnp.log1p(bin_sums)
    shaped = terms.reshape(terms.shape[:-2] + (-1, QLEN, PSG_DEV))
    return LOGIT_GAIN * jnp.sum(shaped, axis=-2)


def expand_tokens(grad_logits):
    return LOGIT_GAIN * jnp.repeat(grad_logits, QLEN, axis=0)


def local_stats(logits, column_ids, wanted):
    positive_hit = (wanted[:, None] == column_ids[None, :]).astype(jnp.float32)
    row_peak = jnp.max(logits, axis=1)
    summed = jnp.sum(jnp.exp(logits - row_peak[:, None]), axis=1)
    chosen = jnp.sum(logits * positive_hit, axis=1)
    return ((row_peak, summed, chosen), positive_hit)


def merge_stats(first, second):
    row_peak = jnp.maximum(first[0], second[0])
    summed = first[1] * jnp.exp(first[0] - row_peak) + second[1] * jnp.exp(second[0] - row_peak)
    return (row_peak, summed, first[2] + second[2])


def finish_loss(logits, merged, positive_hit):
    log_norm = merged[0] + jnp.log(merged[1])
    losses = log_norm - merged[2]
    grad_logits = jnp.exp(logits - log_norm[:, None]) - positive_hit
    return (losses, grad_logits)


def passage_tile_grads(block_queries, passage_tiles, code_tiles, sum_tiles, grad_tiles, exp_tiles):

    def tile_step(running, packed):
        passage_part, code_part, bin_sums, grad_part, exp_sim = packed
        member = bin_members(code_part)
        grad_query, grad_passage = tile_backward(
            exp_sim, member, bin_sums, expand_tokens(grad_part), block_queries, passage_part
        )
        return (running + grad_query, grad_passage)

    step_inputs = (passage_tiles, code_tiles, sum_tiles, grad_tiles, exp_tiles)
    return lax.scan(tile_step, jnp.zeros((block_queries.shape[0], PROJ), jnp.float32), step_inputs)


def passage_tile_sums(block_queries, passage_tiles, code_tiles):

    def tile_sums(packed):
        passage_part, code_part = packed
        return tile_forward(block_queries, passage_part, bin_members(code_part))

    exp_tiles, sum_tiles = lax.map(tile_sums, (passage_tiles, code_tiles))
    return (exp_tiles, sum_tiles)


def body(
    query_states,
    passage_states,
    passage_bins,
    padding_mask,
    token_ids,
    positives,
    united_weight,
    output_weight,
    first_gain,
    first_shift,
    up_weight,
    up_bias,
    down_weight,
    second_gain,
    second_shift,
    project_weight,
):
    query_count = query_states.shape[0]
    all_rows = jnp.concatenate([query_states, passage_states], axis=0)
    united_rows = jnp.dot(all_rows, united_weight, preferred_element_type=jnp.float32).astype(
        jnp.bfloat16
    )
    query_index = lax.broadcasted_iota(jnp.int32, (query_count, query_count), 0) // QLEN
    query_allowed = query_index == jnp.transpose(query_index)
    bins_row = passage_bins[0]
    mask_row = padding_mask[0]
    token_count = bins_row.shape[0]
    diagonal = lax.broadcasted_iota(
        jnp.int32, (token_count, token_count), 0
    ) == lax.broadcasted_iota(jnp.int32, (token_count, token_count), 1)
    passage_allowed = (bins_row[:, None] == bins_row[None, :]) & (
        (mask_row[None, :] == 1) | diagonal
    )
    query_attended, query_log_total = attend_forward(united_rows[:query_count], query_allowed)
    passage_attended, passage_log_total = attend_forward(united_rows[query_count:], passage_allowed)
    attended = jnp.concatenate([query_attended, passage_attended], axis=0)
    hidden_one = all_rows.astype(jnp.float32) + jnp.dot(
        attended, output_weight, preferred_element_type=jnp.float32
    )
    norm_one = layer_norm(hidden_one, first_gain, first_shift)
    norm_one_low = norm_one.astype(jnp.bfloat16)
    up_rows = jnp.dot(norm_one_low, up_weight, preferred_element_type=jnp.float32) + up_bias
    active_low = exact_gelu(up_rows).astype(jnp.bfloat16)
    hidden_two = norm_one + jnp.dot(active_low, down_weight, preferred_element_type=jnp.float32)
    norm_two = layer_norm(hidden_two, second_gain, second_shift)
    norm_two_low = norm_two.astype(jnp.bfloat16)
    projected = jnp.dot(norm_two_low, project_weight, preferred_element_type=jnp.float32)
    embedded = unit_rows(projected)
    embedded_low = embedded.astype(jnp.bfloat16)
    query_emb = embedded_low[:query_count]
    passage_emb = embedded_low[query_count:]
    usable = (mask_row == 1) & (token_ids[0] >= SKIP_IDS)
    own_codes = jnp.where(usable, bins_row, -1)
    narrow_count = lax.axis_size("pa")
    wide_count = lax.axis_size("pb")
    narrow_index = lax.axis_index("pa")
    wide_index = lax.axis_index("pb")
    group_queries = QRY_DEV * narrow_count
    slot_ids = lax.broadcasted_iota(jnp.int32, (1, PSG_DEV), 1)
    block_queries = lax.all_gather(query_emb, "pa", axis=0, tiled=True)
    gathered, gathered_codes = (
        lax.all_gather(passage_emb, "pb", axis=0, tiled=True),
        lax.all_gather(own_codes.astype(jnp.bfloat16)[None, :], "pb", axis=0, tiled=True),
    )
    passage_tiles = gathered.reshape(wide_count, token_count, PROJ)
    code_tiles = gathered_codes.astype(jnp.int32)
    exp_tiles, sum_tiles = passage_tile_sums(block_queries, passage_tiles, code_tiles)
    tile_logits = query_logits(sum_tiles)
    logits = jnp.transpose(tile_logits, (1, 0, 2)).reshape(group_queries, wide_count * PSG_DEV)
    shard_ids = lax.broadcasted_iota(jnp.int32, (wide_count, 1), 0)
    column_ids = ((shard_ids * narrow_count + narrow_index) * PSG_DEV + slot_ids).reshape(-1)
    wanted = lax.dynamic_slice_in_dim(positives, wide_index * group_queries, group_queries)
    stats, positive_hit = local_stats(logits, column_ids, wanted)
    merged = merged_2(stats, "pa", merge_stats)
    losses, grad_logits = finish_loss(logits, merged, positive_hit)
    own_losses = lax.dynamic_slice_in_dim(losses, narrow_index * QRY_DEV, QRY_DEV)
    grad_tiles = jnp.transpose(grad_logits.reshape(group_queries, wide_count, PSG_DEV), (1, 0, 2))
    block_grad, passage_grad_tiles = passage_tile_grads(
        block_queries, passage_tiles, code_tiles, sum_tiles, grad_tiles, exp_tiles
    )
    grad_query_emb = lax.psum_scatter(
        block_grad.astype(jnp.bfloat16), "pa", scatter_dimension=0, tiled=True
    ).astype(jnp.float32)
    grad_passage_emb = lax.psum_scatter(
        passage_grad_tiles.reshape(-1, PROJ), "pb", scatter_dimension=0, tiled=True
    )
    grad_embedded = jnp.concatenate([grad_query_emb, grad_passage_emb], axis=0)
    unit_pull = jax.vjp(unit_rows, projected)[1]
    grad_projected = unit_pull(grad_embedded)[0].astype(jnp.bfloat16)
    grad_project = contract_rows(norm_two_low, grad_projected)
    grad_norm_two = times_transposed(grad_projected, project_weight)
    second_pull = jax.vjp(layer_norm, hidden_two, second_gain, second_shift)[1]
    grad_hidden_two, grad_second_gain, grad_second_shift = second_pull(grad_norm_two)
    grad_branch_two = grad_hidden_two.astype(jnp.bfloat16)
    grad_down = contract_rows(active_low, grad_branch_two)
    grad_active = times_transposed(grad_branch_two, down_weight)
    gelu_pull = jax.vjp(exact_gelu, up_rows)[1]
    grad_up_rows = gelu_pull(grad_active)[0].astype(jnp.bfloat16)
    grad_up_bias = jnp.sum(grad_up_rows, axis=0, dtype=jnp.float32)
    grad_up = contract_rows(norm_one_low, grad_up_rows)
    grad_norm_one = times_transposed(grad_up_rows, up_weight) + grad_hidden_two
    first_pull = jax.vjp(layer_norm, hidden_one, first_gain, first_shift)[1]
    grad_hidden_one, grad_first_gain, grad_first_shift = first_pull(grad_norm_one)
    grad_branch_one = grad_hidden_one.astype(jnp.bfloat16)
    grad_output = contract_rows(attended, grad_branch_one)
    grad_attended = times_transposed(grad_branch_one, output_weight).astype(jnp.bfloat16)
    grad_query_united = attend_backward(
        united_rows[:query_count], query_allowed, query_log_total, grad_attended[:query_count]
    )
    grad_passage_united = attend_backward(
        united_rows[query_count:], passage_allowed, passage_log_total, grad_attended[query_count:]
    )
    grad_united_rows = jnp.concatenate([grad_query_united, grad_passage_united], axis=0)
    grad_united = contract_rows(all_rows, grad_united_rows)
    grad_rows = times_transposed(grad_united_rows, united_weight) + grad_hidden_one
    shared = (
        lax.psum_scatter(grad_united, ("pb", "pa"), scatter_dimension=0, tiled=True),
        lax.psum_scatter(grad_output, ("pb", "pa"), scatter_dimension=0, tiled=True),
        lax.psum_scatter(grad_first_gain, ("pb", "pa"), scatter_dimension=0, tiled=True),
        lax.psum_scatter(grad_first_shift, ("pb", "pa"), scatter_dimension=0, tiled=True),
        lax.psum_scatter(grad_up, ("pb", "pa"), scatter_dimension=0, tiled=True),
        lax.psum_scatter(grad_up_bias, ("pb", "pa"), scatter_dimension=0, tiled=True),
        lax.psum_scatter(grad_down, ("pb", "pa"), scatter_dimension=0, tiled=True),
        lax.psum_scatter(grad_second_gain, ("pb", "pa"), scatter_dimension=0, tiled=True),
        lax.psum_scatter(grad_second_shift, ("pb", "pa"), scatter_dimension=0, tiled=True),
        lax.psum_scatter(grad_project, ("pb", "pa"), scatter_dimension=0, tiled=True),
    )
    return (
        query_emb,
        passage_emb,
        own_losses,
        grad_rows[:query_count],
        grad_rows[query_count:],
        shared[0],
        shared[1],
        shared[2],
        shared[3],
        shared[4],
        shared[5],
        shared[6],
        shared[7],
        shared[8],
        shared[9],
    )


def solution(mesh):
    return jax.shard_map(
        body,
        mesh=mesh,
        in_specs=(
            P(("pb", "pa"), None),
            P(("pb", "pa"), None),
            P(("pb", "pa"), None),
            P(("pb", "pa"), None),
            P(("pb", "pa"), None),
            P(),
            P(),
            P(),
            P(),
            P(),
            P(),
            P(),
            P(),
            P(),
            P(),
            P(),
        ),
        out_specs=(
            P(("pb", "pa"), None),
            P(("pb", "pa"), None),
            P(("pb", "pa")),
            P(("pb", "pa"), None),
            P(("pb", "pa"), None),
            P(("pb", "pa"), None),
            P(("pb", "pa"), None),
            P(("pb", "pa")),
            P(("pb", "pa")),
            P(("pb", "pa"), None),
            P(("pb", "pa")),
            P(("pb", "pa"), None),
            P(("pb", "pa")),
            P(("pb", "pa")),
            P(("pb", "pa"), None),
        ),
        check_vma=False,
    )
```

profile of v0, /device:TPU:0, one launch (start us, length us, event | category | flops | bytes accessed | tf_op | source)
XLA Modules:
  0.0 1116.8 jit_solution(4050556156255983791)
XLA Ops:
  10.7 3.3 convolution_convert_fusion
  17.8 5.8 copy.84
  24.7 13.3 %fusion.24 = (f32[12,768]{1,0:T(8,128)S(1)}, f32[12,768,768]{1,2,0:T(8,128)}) fusion(pred[768,768]{0,1:T(8,128)(4,1)S(1)} %fusion.35, bf16[768,3,12,64]{0,3,2,1:T(8,128)(2,1)} %bitcast.201), kind=kOutput, calls=%fused_computation.45 | convolution fusion | flops 927194112 | bytes 31297536 | tf_op jit(solution)/shard_map/qhd,khd->hqk/dot_general | solution.py:65
  38.0 12.7 %exponential_reduce_fusion = f32[12,768]{1,0:T(8,128)S(1)} fusion(f32[12,768,768]{1,2,0:T(8,128)} %get-tuple-element.417, f32[12,768]{1,0:T(8,128)S(1)} %get-tuple-element.416, pred[768,768]{0,1:T(8,128)(4,1)S(1)} %fusion.35), kind=kLoop, calls=%fused_computation.43 | loop fusion | flops 28302336 | bytes 28975104 | tf_op jit(solution)/shard_map/reduce_sum | solution.py:75
  51.3 14.0 %convolution_convert_fusion.3 = bf16[12,64,768]{2,1,0:T(8,128)(2,1)} fusion(bf16[768,3,12,64]{0,3,2,1:T(8,128)(2,1)} %bitcast.202, f32[12,768,768]{1,2,0:T(8,128)} %get-tuple-element.417, f32[12,768]{1,0:T(8,128)S(1)} %log_add_fusion, pred[768,768]{0,1:T(8,128)(4,1)S(1)} %fusion.35), kind=kOutput, calls=%fused_computation.94 | convolution fusion | flops 934871040 | bytes 31297536 | tf_op jit(solution)/shard_map/hqk,khd->qhd/dot_general | solution.py:77
  65.4 2.4 reshape.357
  74.2 3.9 fusion.85
  79.6 29.7 %multiply_convert_fusion.1 = (bf16[832,3072]{1,0:T(8,128)(2,1)S(1)}, f32[832,3072]{1,0:T(8,128)}, f32[832,3072]{1,0:T(8,128)}) fusion(f32[3072]{0:T(1024)S(1)} %copy-done.68, bf16[768,3072]{1,0:T(8,128)(2,1)} %param.32, f32[832,768]{1,0:T(8,128)S(1)} %get-tuple-element.421, f32[768]{0:T(1024)S(1)} %copy-done.35, f32[768]{0:T(1024)S(1)} %copy-done.30, ...), kind=kOutput, calls=%fused_computation.51 | convolution fusion | flops 4097753088 | bytes 32858624 | tf_op jit(solution)/shard_map/dot_general | solution.py:226
  109.3 4.4 fusion.86
  119.9 10.7 all-gather.3
  134.4 14.1 %all_gather.28 = bf16[256,128]{1,0:T(8,128)(2,1)} all-gather(bf16[64,128]{1,0:T(8,128)(2,1)S(1)} %slice.78), channel_id=1, replica_groups=mesh['pb'=8,'pa'=4] {'pa'}, dimensions={0}, use_global_device_ids=true | all-gather | bytes 81920 | tf_op jit(solution)/shard_map/all_gather | solution.py:244
  149.1 32.4 %while.44 = (s32[]{:T(128)}, f32[8,256,768]{1,2,0:T(8,128)}, f32[8,256,4]{1,2,0:T(4,128)}, bf16[8,768,128]{2,1,0:T(8,128)(2,1)}, bf16[256,128]{1,0:T(8,128)(2,1)}, /*index=5*/s32[8,768]{1,0:T(8,128)}, s32[]{:T(128)}) while((s32[]{:T(128)}, f32[8,256,768]{1,2,0:T(8,128)}, f32[8,256,4]{1,2,0:T(4,128)}, bf16[8,768,128]{2,1,0:T(8,128)(2,1)}, ...), condition=%wide.region_10.11_spmd, body=%wide.region_9.10_spmd.sunk | while | flops 59968512 | bytes 2636369 | solution.py:180
  149.1 2.1 bitcast_dynamic-update-slice_fusion.2
  153.2 2.1 bitcast_dynamic-update-slice_fusion.2
  157.2 2.1 bitcast_dynamic-update-slice_fusion.2
  161.3 2.1 bitcast_dynamic-update-slice_fusion.2
  165.3 2.1 bitcast_dynamic-update-slice_fusion.2
  169.4 2.1 bitcast_dynamic-update-slice_fusion.2
  173.4 2.2 bitcast_dynamic-update-slice_fusion.2
  177.5 2.1 bitcast_dynamic-update-slice_fusion.2
  192.8 12.4 %all-reduce.10 = (f32[32]{0:T(128)}, f32[32]{0:T(128)}, f32[32]{0:T(128)}) all-reduce(f32[32]{0:T(128)} %dynamic-update-slice, f32[32]{0:T(128)} %dynamic-update-slice.1, f32[32]{0:T(128)} %dynamic-update-slice.2), channel_id=2, replica_groups=mesh['pb'=8,'pa'=4] {'pa'}, use_global_device_ids=true, to_apply=%add | all-reduce | flops 96 | bytes 768
  209.2 3.8 while.45
  215.6 104.6 %while.46 = (s32[]{:T(128)}, f32[256,128]{1,0:T(8,128)}, f32[8,768,128]{2,1,0:T(8,128)}, f32[8,256,768]{1,2,0:T(8,128)}, f32[8,8,4]{1,2,0:T(4,128)}, /*index=5*/...) while((s32[]{:T(128)}, f32[256,128]{1,0:T(8,128)}, ...), condition=%wide.region_18.19_spmd.clone, body=%wide.region_17.18_spmd.clone.sunk | while | flops 110564384 | bytes 7633951 | solution.py:171
  215.6 2.1 constant_dynamic-slice_fusion.5
  217.7 2.3 copy.139
  228.6 2.1 constant_dynamic-slice_fusion.5
  230.7 2.3 copy.139
  241.7 2.1 constant_dynamic-slice_fusion.5
  243.8 2.3 copy.139
  254.8 2.1 constant_dynamic-slice_fusion.5
  256.9 2.3 copy.139
  267.9 2.1 constant_dynamic-slice_fusion.5
  269.9 2.3 copy.139
  281.0 2.1 constant_dynamic-slice_fusion.5
  283.0 2.3 copy.139
  294.0 2.1 constant_dynamic-slice_fusion.5
  296.1 2.3 copy.139
  307.1 2.1 constant_dynamic-slice_fusion.5
  309.2 2.3 copy.139
  318.2 2.0 convolution_add_fusion.2
  322.6 15.8 %reduce-scatter.10.cloned.1.call-done = bf16[64,128]{1,0:T(8,128)(2,1)} async-done(((bf16[256,128]{1,0:T(8,128)(2,1)}), bf16[64,128]{1,0:T(8,128)(2,1)}) %reduce-scatter.10.cloned.1.call-update) | async-done | bytes 16400 | tf_op jit(solution)/shard_map/reduce_scatter | solution.py:265
  339.7 46.3 %reduce-scatter.12.cloned.1.call-done = f32[768,128]{1,0:T(8,128)} async-done(((f32[6144,128]{1,0:T(8,128)}), f32[768,128]{1,0:T(8,128)}) %reduce-scatter.12.cloned.1.call-update) | async-done | bytes 393232 | tf_op jit(solution)/shard_map/reduce_scatter | solution.py:268
  390.3 3.5 multiply_reduce_fusion.1
  393.8 2.3 fusion.80
  396.2 17.1 %convert_reduce_fusion = (f32[3072]{0:T(1024)}, bf16[832,3072]{1,0:T(8,128)(2,1)}) fusion(f32[832,3072]{1,0:T(8,128)} %get-tuple-element.407, bf16[3072,768]{1,0:T(8,128)(2,1)} %param.34, f32[832,768]{1,0:T(8,128)} %get-tuple-element.403, f32[832]{0:T(1024)S(1)} %negate_multiply_fusion.2, f32[832,3072]{1,0:T(8,128)} %get-tuple-element.422, ...), kind=kOutput, calls=%fused_computation.49 | convolution fusion | flops 3970593792 | bytes 32861440 | tf_op jit(solution)/shard_map/re,de->rd/dot_general | solution.py:55
  413.4 10.1 multiply_reduce_fusion.2
  427.8 2.4 copy.99
  430.1 24.8 %multiply_reduce_fusion = (f32[12,768]{1,0:T(8,128)}, f32[12,768,768]{1,2,0:T(8,128)}) fusion(f32[12,768,768]{1,2,0:T(8,128)} %get-tuple-element.417, f32[12,768]{1,0:T(8,128)} %copy-done.24, pred[768,768]{0,1:T(8,128)(4,1)} %copy-done.6, bf16[768,12,64]{0,2,1:T(8,128)(2,1)} %bitcast.206, bf16[768,3,12,64]{0,3,2,1:T(8,128)(2,1)} %bitcast.203), kind=kOutput, calls=%fused_computation.41 | convolution fusion | flops 941349888 | bytes 59658240 | tf_op jit(solution)/shard_map/qhd,khd->hqk/dot_general | solution.py:86
  454.9 23.6 %multiply_convert_fusion = bf16[12,768,768]{1,2,0:T(8,128)(2,1)} fusion(f32[12,768,768]{1,2,0:T(8,128)} %get-tuple-element.430, f32[12,768,768]{1,2,0:T(8,128)} %get-tuple-element.417, f32[12,768]{1,0:T(8,128)} %get-tuple-element.429, f32[12,768]{1,0:T(8,128)} %copy-done.24, pred[768,768]{0,1:T(8,128)(4,1)} %copy-done.6), kind=kLoop, calls=%fused_computation.40 | loop fusion | flops 42467328 | bytes 71442432 | tf_op jit(solution)/shard_map/convert_element_type | solution.py:90
  478.5 9.0 fusion.39
  487.5 10.9 fusion.40
  501.6 2.8 multiply_reduce_fusion.9
  504.4 5.2 fusion.49
  515.6 2.1 copy.118
  517.7 14.4 %fusion.38 = bf16[768,1,12,64]{0,3,2,1:T(8,128)(2,1)} fusion(bf16[768,12,64]{0,2,1:T(8,128)(2,1)} %bitcast.207, f32[12,768,768]{1,2,0:T(8,128)} %get-tuple-element.417, f32[12,768]{1,0:T(8,128)} %copy-done.24, pred[768,768]{0,1:T(8,128)(4,1)} %copy-done.6), kind=kOutput, calls=%fused_computation.95 | convolution fusion | flops 934871040 | bytes 31297536 | tf_op jit(solution)/shard_map/hqk,qhd->khd/dot_general | solution.py:99
  535.5 8.2 fusion.32
  544.4 10.2 fusion.72
  555.3 10.9 fusion.74
  567.4 7.6 add_add_fusion.2
  577.3 40.3 %all-reduce.9 = (f32[768]{0:T(1024)}, f32[768]{0:T(1024)}, f32[3072]{0:T(1024)}, f32[768]{0:T(1024)}, f32[768]{0:T(1024)}) all-reduce(f32[768]{0:T(1024)S(1)} %copy-done.54, f32[768]{0:T(1024)S(1)} %copy-done.55, f32[3072]{0:T(1024)} %get-tuple-element.433, ...), channel_id=9, replica_groups=mesh['pb'=8,'pa'=4] {'pb','pa'}, use_global_device_ids=true, to_apply=%region_31.32.clone | all-reduce | flops 6144 | bytes 49152
  624.0 77.5 %reduce-scatter.16.cloned.1.call-done = f32[24,768]{1,0:T(8,128)} async-done(((f32[768,768]{1,0:T(8,128)}), f32[24,768]{1,0:T(8,128)}) %reduce-scatter.16.cloned.1.call-update) | async-done | bytes 73744 | tf_op jit(solution)/shard_map/reduce_scatter | solution.py:302
  701.5 124.8 %reduce-scatter.14.cloned.1.call-done = f32[24,2304]{1,0:T(8,128)} async-done(((f32[768,2304]{1,0:T(8,128)}), f32[24,2304]{1,0:T(8,128)}) %reduce-scatter.14.cloned.1.call-update) | async-done | bytes 221200 | tf_op jit(solution)/shard_map/reduce_scatter | solution.py:301
  826.3 141.6 %reduce-scatter.20.cloned.1.call-done = f32[96,768]{1,0:T(8,128)} async-done(((f32[3072,768]{1,0:T(8,128)}), f32[96,768]{1,0:T(8,128)}) %reduce-scatter.20.cloned.1.call-update) | async-done | bytes 294928 | tf_op jit(solution)/shard_map/reduce_scatter | solution.py:307
  967.9 141.6 %reduce-scatter.18.cloned.1.call-done = f32[24,3072]{1,0:T(8,128)} async-done(((f32[768,3072]{1,0:T(8,128)}), f32[24,3072]{1,0:T(8,128)}) %reduce-scatter.18.cloned.1.call-update) | async-done | bytes 294928 | tf_op jit(solution)/shard_map/reduce_scatter | solution.py:305
  (337 shorter events, 167.2 us)
Async XLA Ops:
  7.2 3.5 copy-start
  7.2 141.9 %all-gather.6.cloned.1.call-start = ((), (), s32[]{:S(2)}) async-start(), calls=%async_computation.7 | async-start | bytes 1769472 | tf_op jit(solution)/shard_map/all_gather | solution.py:246
  9.6 1.0 copy-start.52
  17.8 5.8 copy-start.51
  17.8 5.8 copy-start.61
  17.8 5.8 copy-start.62
  24.7 26.0 %copy-start.6 = (pred[768,768]{0,1:T(8,128)(4,1)}, pred[768,768]{0,1:T(8,128)(4,1)S(1)}, u32[]{:S(2)}) copy-start(pred[768,768]{0,1:T(8,128)(4,1)S(1)} %fusion.35) | copy-start | bytes 1769476
  51.3 18.4 %copy-start.64 = (s32[64]{0:T(128)S(1)}, s32[64]{0:T(128)}, u32[]{:S(2)}) copy-start(s32[64]{0:T(128)} %get-tuple-element.436) | copy-start | bytes 772
  51.3 18.4 %copy-start.65 = (pred[64]{0:T(512)(128)(4,1)S(1)}, pred[64]{0:T(512)(128)(4,1)}, u32[]{:S(2)}) copy-start(pred[64]{0:T(512)(128)(4,1)} %compare_and_fusion) | copy-start | bytes 196
  69.7 1.2 copy-start.18
  69.7 1.3 copy-start.19
  70.9 7.1 copy-start.27
  74.1 4.0 copy-start.29
  74.1 5.4 copy-start.30
  74.1 5.4 copy-start.35
  74.1 5.4 copy-start.68
  74.2 35.1 %slice-start = ((s8[4718592]{0:T(1024)(128)(4,1)}), s8[4194304]{0:T(1024)(128)(4,1)S(1)}, s32[]{:S(2)}) async-start(s8[4718592]{0:T(1024)(128)(4,1)} %bitcast.222), calls=%async_computation.15 | async-start | bytes 8388608
  78.1 31.2 %copy-start.4 = (f32[832,768]{1,0:T(8,128)}, f32[832,768]{1,0:T(8,128)S(1)}, u32[]{:S(2)}) copy-start(f32[832,768]{1,0:T(8,128)S(1)} %get-tuple-element.421) | copy-start | bytes 7667716
  78.1 31.1 %copy-start.22 = (f32[832]{0:T(1024)}, f32[832]{0:T(1024)S(1)}, u32[]{:S(2)}) copy-start(f32[832]{0:T(1024)S(1)} %broadcast_multiply_fusion.1) | copy-start | bytes 9988
  79.6 29.7 %copy-start.25 = (f32[832]{0:T(1024)}, f32[832]{0:T(1024)S(1)}, u32[]{:S(2)}) copy-start(f32[832]{0:T(1024)S(1)} %fusion.62) | copy-start | bytes 9988
  79.6 29.7 %slice-start.1 = ((s8[4718592]{0:T(1024)(128)(4,1)}), s8[524288]{0:T(1024)(128)(4,1)S(1)}, s32[]{:S(2)}) async-start(s8[4718592]{0:T(1024)(128)(4,1)} %bitcast.222), calls=%async_computation.16 | async-start | bytes 1048576
  109.2 4.5 copy-start.70
  109.3 6.1 copy-start.40
  109.3 6.1 copy-start.60
  113.8 2.7 copy-start.2
  113.8 2.1 copy-start.20
  115.9 1.1 copy-start.7
  119.1 219.3 %reduce-scatter.10.cloned.1.call-start = ((), (), s32[]{:S(2)}) async-start(), calls=%async_computation.8 | async-start | bytes 81920 | tf_op jit(solution)/shard_map/reduce_scatter | solution.py:265
  119.9 29.3 %copy-start.39 = (bf16[64,128]{1,0:T(8,128)(2,1)}, bf16[64,128]{1,0:T(8,128)(2,1)S(1)}, u32[]{:S(2)}) copy-start(bf16[64,128]{1,0:T(8,128)(2,1)S(1)} %slice.78) | copy-start | bytes 49156
  320.2 68.0 %copy-start.43 = (f32[832]{0:T(1024)S(1)}, f32[832]{0:T(1024)}, u32[]{:S(2)}) copy-start(f32[832]{0:T(1024)} %copy-done.42) | copy-start | bytes 9988
  320.2 70.1 %copy-start.34 = (f32[832]{0:T(1024)S(1)}, f32[832]{0:T(1024)}, u32[]{:S(2)}) copy-start(f32[832]{0:T(1024)} %copy-done.33) | copy-start | bytes 9988
  320.2 70.1 %copy-start.38 = (f32[832]{0:T(1024)S(1)}, f32[832]{0:T(1024)}, u32[]{:S(2)}) copy-start(f32[832]{0:T(1024)} %copy-done.37) | copy-start | bytes 9988
  320.2 70.1 %copy-start.41 = (f32[768]{0:T(1024)S(1)}, f32[768]{0:T(1024)}, u32[]{:S(2)}) copy-start(f32[768]{0:T(1024)} %param.35) | copy-start | bytes 9220
  321.8 64.2 %reduce-scatter.12.cloned.1.call-start = ((), (), s32[]{:S(2)}) async-start(), calls=%async_computation.9 | async-start | bytes 3538944 | tf_op jit(solution)/shard_map/reduce_scatter | solution.py:268
  322.5 301.5 %reduce-scatter.22.cloned.1.call-start = ((), (), s32[]{:S(2)}) async-start(), calls=%async_computation.14 | async-start | bytes 405504
  386.0 7.8 copy-start.47
  386.0 7.8 copy-start.3
  393.8 2.4 copy-start.69
  396.2 17.2 %copy-start.58 = (f32[832]{0:T(1024)}, f32[832]{0:T(1024)S(1)}, u32[]{:S(2)}) copy-start(f32[832]{0:T(1024)S(1)} %negate_multiply_fusion.2) | copy-start | bytes 9988
  396.2 17.2 %copy-start.5 = (f32[832,768]{1,0:T(8,128)S(1)}, f32[832,768]{1,0:T(8,128)}, u32[]{:S(2)}) copy-start(f32[832,768]{1,0:T(8,128)} %copy-done.4) | copy-start | bytes 7667716
  396.2 17.2 %copy-start.23 = (f32[832]{0:T(1024)S(1)}, f32[832]{0:T(1024)}, u32[]{:S(2)}) copy-start(f32[832]{0:T(1024)} %copy-done.22) | copy-start | bytes 9988
  396.2 17.2 %copy-start.26 = (f32[832]{0:T(1024)S(1)}, f32[832]{0:T(1024)}, u32[]{:S(2)}) copy-start(f32[832]{0:T(1024)} %copy-done.25) | copy-start | bytes 9988
  396.2 17.2 %copy-start.31 = (f32[768]{0:T(1024)S(1)}, f32[768]{0:T(1024)}, u32[]{:S(2)}) copy-start(f32[768]{0:T(1024)} %param.30) | copy-start | bytes 9220
  413.4 10.1 copy-start.45
  423.5 1.3 copy-start.67
  424.4 1.5 copy-start.14
  424.4 1.5 copy-start.56
  487.5 10.9 copy-start.8
  487.5 10.9 copy-start.16
  487.5 14.1 %copy-start.28 = (f32[12,64]{1,0:T(8,128)S(1)}, f32[12,64]{1,0:T(8,128)}, u32[]{:S(2)}) copy-start(f32[12,64]{1,0:T(8,128)} %copy-done.27) | copy-start | bytes 9220
  501.5 200.0 %reduce-scatter.16.cloned.1.call-start = ((), (), s32[]{:S(2)}) async-start(), calls=%async_computation.11 | async-start | bytes 2433024 | tf_op jit(solution)/shard_map/reduce_scatter | solution.py:302
  509.6 316.7 %reduce-scatter.14.cloned.1.call-start = ((), (), s32[]{:S(2)}) async-start(), calls=%async_computation.10 | async-start | bytes 7299072 | tf_op jit(solution)/shard_map/reduce_scatter | solution.py:301
  517.7 14.4 %copy-start.11 = (bf16[768,1,12,64]{0,3,2,1:T(8,128)(2,1)S(1)}, bf16[768,1,12,64]{0,3,2,1:T(8,128)(2,1)}, u32[]{:S(2)}) copy-start(bf16[768,1,12,64]{0,3,2,1:T(8,128)(2,1)} %fusion.40) | copy-start | bytes 3538948
  517.7 14.4 %copy-start.12 = (bf16[768,1,12,64]{0,3,2,1:T(8,128)(2,1)S(1)}, bf16[768,1,12,64]{0,3,2,1:T(8,128)(2,1)}, u32[]{:S(2)}) copy-start(bf16[768,1,12,64]{0,3,2,1:T(8,128)(2,1)} %fusion.39) | copy-start | bytes 3538948
  532.1 3.4 copy-start.21
  532.1 3.4 copy-start.53
  533.7 1.8 copy-start.13
  543.7 424.2 %reduce-scatter.20.cloned.1.call-start = ((), (), s32[]{:S(2)}) async-start(), calls=%async_computation.13 | async-start | bytes 9732096 | tf_op jit(solution)/shard_map/reduce_scatter | solution.py:307
  554.6 554.9 %reduce-scatter.18.cloned.1.call-start = ((), (), s32[]{:S(2)}) async-start(), calls=%async_computation.12 | async-start | bytes 9732096 | tf_op jit(solution)/shard_map/reduce_scatter | solution.py:305
  566.2 1.2 copy-start.57
  575.0 2.3 copy-start.49
  575.1 2.3 copy-start.50
  575.1 2.3 copy-start.54
  575.1 2.3 copy-start.55
  (24 other events, 16.9 us)
Sparse Core Ops, SparseCore 0:
  119.2 28.2 all-gather.5
  321.9 16.4 reduce-scatter.9
  341.8 44.2 reduce-scatter.11
  501.6 95.5 reduce-scatter.21
  602.9 98.6 reduce-scatter.15
  707.6 118.6 reduce-scatter.13
  832.8 135.1 reduce-scatter.19
  974.4 135.1 reduce-scatter.17
where the time goes:
time: 1130 us; the launch traced here: 1120 us
  waiting for transfers between devices  548 us (48%)
  matrix products  284 us (25%)
  local copies, waits for them, and re-layouts  120 us (11%)
  blocking collectives  77.5 us (7%)
  other arithmetic  70.1 us (6%)
  between operations  16 us (1%)
    reduce_scatter x1, waiting for transfers between devices, body(): lax.psum_scatter(grad_down, ('pb', 'pa'), scatter_dimension=0, tiled=True)  142 us
    reduce_scatter x1, waiting for transfers between devices, body(): lax.psum_scatter(grad_up, ('pb', 'pa'), scatter_dimension=0, tiled=True)  142 us
    reduce_scatter x1, waiting for transfers between devices, body(): lax.psum_scatter(grad_united, ('pb', 'pa'), scatter_dimension=0, tiled=True)  125 us
    reduce_scatter x1, waiting for transfers between devices, body(): lax.psum_scatter(grad_output, ('pb', 'pa'), scatter_dimension=0, tiled=True)  77.5 us
    unnamed x2, blocking collectives  52.7 us
    reduce_scatter x1, waiting for transfers between devices, body(): lax.psum_scatter(passage_grad_tiles.reshape(-1, PROJ), 'pb', scatter_dime...  46.3 us
    dot_general x5, matrix products, times_transposed(): jnp.einsum('re,de->rd', operand, partner, preferred_element_type=jnp.floa...  39.5 us
    dot_general x5, matrix products, contract_rows(): jnp.einsum('rd,re->de', operand, partner, preferred_element_type=jnp.floa...  35.8 us
  transfers between devices with their start and end apart: 8, of which 6 were waited for; matrix products, arithmetic and copies ran while one was open for 8% of the time, Pallas kernels for 0%

commit v1 on v0

--- a/solution.py
+++ b/solution.py
@@ -1,6 +1,8 @@
 import jax
 import jax.numpy as jnp
 from jax import lax
+from jax.experimental import pallas as pl
+from jax.experimental.pallas import tpu as pltpu
 from jax.sharding import PartitionSpec as P
 
 D = 768
@@ -8,9 +10,10 @@
 HEADS = 12
 PROJ = 128
 QLEN = 32
-QRY_DEV = 2
 PSG_DEV = 4
 SKIP_IDS = 3000
+LANES = 128
+TILE = 256
 
 
 SOFT_TEMP = 0.1
@@ -20,17 +23,6 @@
 SCORE_SCALE = 0.125
 
 
-def merged_2(part, axis, combine):
-    gathered = jax.tree.map(lambda a: lax.all_gather(a, axis), part)
-
-    def take(source):
-        return jax.tree.map(lambda a: lax.dynamic_index_in_dim(a, source, 0, False), gathered)
-
-    return lax.fori_loop(
-        1, lax.axis_size(axis), lambda source, state: combine(state, take(source)), take(0)
-    )
-
-
 def layer_norm(hidden, gain_row, shift_row):
     centred = hidden - jnp.mean(hidden, axis=-1, keepdims=True)
     spread = jnp.mean(centred * centred, axis=-1, keepdims=True)
@@ -48,7 +40,8 @@
 
 
 def contract_rows(operand, partner):
-    return jnp.einsum("rd,re->de", operand, partner, preferred_element_type=jnp.float32)
+    summed = jnp.einsum("rd,re->de", operand, partner, preferred_element_type=jnp.float32)
+    return summed.astype(jnp.bfloat16)
 
 
 def times_transposed(operand, partner):
@@ -103,82 +96,142 @@
     return joined.reshape(united_rows.shape[0], 3 * D).astype(jnp.bfloat16)
 
 
-def bin_members(codes):
-    slot_ids = lax.broadcasted_iota(jnp.int32, (codes.shape[0], PSG_DEV), 1)
-    return (codes[:, None] == slot_ids).astype(jnp.float32)
-
-
-def tile_forward(query_part, passage_part, member):
-    similarity = jnp.einsum(
-        "te,pe->tp", query_part, passage_part, preferred_element_type=jnp.float32
-    )
-    exp_sim = jnp.exp(similarity / SOFT_TEMP)
-    bin_sums = jnp.dot(exp_sim, member, precision=lax.Precision.HIGHEST)
-    return (exp_sim, bin_sums)
-
-
-def tile_backward(exp_sim, member, bin_sums, grad_bins, query_part, passage_part):
-    weight_bins = grad_bins / (1.0 + bin_sums)
-    spread = jnp.dot(weight_bins, jnp.transpose(member), precision=lax.Precision.HIGHEST)
+def member_rows(code_row):
+    slot_ids = lax.broadcasted_iota(jnp.int32, (LANES, code_row.shape[-1]), 0)
+    return (code_row == slot_ids).astype(jnp.float32).astype(jnp.bfloat16)
+
+
+def split_low(values):
+    high = values.astype(jnp.bfloat16)
+    return high, (values - high.astype(jnp.float32)).astype(jnp.bfloat16)
+
+
+def exp_similarity(query_tile, passage_rows):
+    similarity = lax.dot_general(
+        query_tile, passage_rows, (((1,), (1,)), ((), ())), preferred_element_type=jnp.float32
+    )
+    return jnp.exp(similarity * (1.0 / SOFT_TEMP))
+
+
+def tile_forward_kernel(query_ref, passage_ref, code_ref, inverse_ref, logit_ref):
+    exp_sim = exp_similarity(query_ref[...], passage_ref[...])
+    member = member_rows(code_ref[...])
+    high, rest = split_low(exp_sim)
+    contract = (((1,), (1,)), ((), ()))
+    bin_sums = lax.dot_general(
+        high, member, contract, preferred_element_type=jnp.float32
+    ) + lax.dot_general(rest, member, contract, preferred_element_type=jnp.float32)
+    inverse_ref[...] = 1.0 / (1.0 + bin_sums)
+    terms = SOFT_TEMP * jnp.log1p(bin_sums)
+    logit_ref[...] = LOGIT_GAIN * jnp.sum(terms.reshape(-1, QLEN, LANES), axis=1)
+
+
+def tile_backward_kernel(
+    query_ref, passage_ref, code_ref, inverse_ref, grad_ref, grad_query_ref, grad_passage_ref
+):
+    exp_sim = exp_similarity(query_ref[...], passage_ref[...])
+    member = member_rows(code_ref[...])
+    grad_tokens = LOGIT_GAIN * jnp.broadcast_to(
+        grad_ref[...][:, None, :], (grad_ref.shape[0], QLEN, LANES)
+    ).reshape(-1, LANES)
+    high, rest = split_low(grad_tokens * inverse_ref[...])
+    spread = jnp.dot(high, member, preferred_element_type=jnp.float32) + jnp.dot(
+        rest, member, preferred_element_type=jnp.float32
+    )
     grad_sim = (exp_sim * spread).astype(jnp.bfloat16)
-    grad_query = jnp.einsum("tp,pe->te", grad_sim, passage_part, preferred_element_type=jnp.float32)
-    grad_passage = jnp.einsum("tp,te->pe", grad_sim, query_part, preferred_element_type=jnp.float32)
-    return (grad_query, grad_passage)
-
-
-def query_logits(bin_sums):
-    terms = SOFT_TEMP * jnp.log1p(bin_sums)
-    shaped = terms.reshape(terms.shape[:-2] + (-1, QLEN, PSG_DEV))
-    return LOGIT_GAIN * jnp.sum(shaped, axis=-2)
-
-
-def expand_tokens(grad_logits):
-    return LOGIT_GAIN * jnp.repeat(grad_logits, QLEN, axis=0)
-
-
-def local_stats(logits, column_ids, wanted):
-    positive_hit = (wanted[:, None] == column_ids[None, :]).astype(jnp.float32)
-    row_peak = jnp.max(logits, axis=1)
-    summed = jnp.sum(jnp.exp(logits - row_peak[:, None]), axis=1)
-    chosen = jnp.sum(logits * positive_hit, axis=1)
-    return ((row_peak, summed, chosen), positive_hit)
-
-
-def merge_stats(first, second):
-    row_peak = jnp.maximum(first[0], second[0])
-    summed = first[1] * jnp.exp(first[0] - row_peak) + second[1] * jnp.exp(second[0] - row_peak)
-    return (row_peak, summed, first[2] + second[2])
-
-
-def finish_loss(logits, merged, positive_hit):
-    log_norm = merged[0] + jnp.log(merged[1])
-    losses = log_norm - merged[2]
-    grad_logits = jnp.exp(logits - log_norm[:, None]) - positive_hit
-    return (losses, grad_logits)
-
-
-def passage_tile_grads(block_queries, passage_tiles, code_tiles, sum_tiles, grad_tiles, exp_tiles):
-
-    def tile_step(running, packed):
-        passage_part, code_part, bin_sums, grad_part, exp_sim = packed
-        member = bin_members(code_part)
-        grad_query, grad_passage = tile_backward(
-            exp_sim, member, bin_sums, expand_tokens(grad_part), block_queries, passage_part
-        )
-        return (running + grad_query, grad_passage)
-
-    step_inputs = (passage_tiles, code_tiles, sum_tiles, grad_tiles, exp_tiles)
-    return lax.scan(tile_step, jnp.zeros((block_queries.shape[0], PROJ), jnp.float32), step_inputs)
-
-
-def passage_tile_sums(block_queries, passage_tiles, code_tiles):
-
-    def tile_sums(packed):
-        passage_part, code_part = packed
-        return tile_forward(block_queries, passage_part, bin_members(code_part))
-
-    exp_tiles, sum_tiles = lax.map(tile_sums, (passage_tiles, code_tiles))
-    return (exp_tiles, sum_tiles)
+    grad_query_ref[...] = jnp.dot(
+        grad_sim, passage_ref[...], preferred_element_type=jnp.float32
+    ).astype(jnp.bfloat16)
+    partial = lax.dot_general(
+        grad_sim, query_ref[...], (((0,), (0,)), ((), ())), preferred_element_type=jnp.float32
+    )
+
+    @pl.when(pl.program_id(0) == 0)
+    def _():
+        grad_passage_ref[...] = jnp.zeros_like(grad_passage_ref)
+
+    grad_passage_ref[...] += partial
+
+
+def tile_specs(token_count):
+    rows = pl.BlockSpec((TILE, LANES), lambda i: (i, 0))
+    fixed = pl.BlockSpec((token_count, PROJ), lambda i: (0, 0))
+    codes = pl.BlockSpec((1, token_count), lambda i: (0, 0))
+    few = pl.BlockSpec((TILE // QLEN, LANES), lambda i: (i, 0))
+    return rows, fixed, codes, few
+
+
+def tile_forward(queries, passages, codes):
+    rows, fixed, code_spec, few = tile_specs(passages.shape[0])
+    count = queries.shape[0]
+    return pl.pallas_call(
+        tile_forward_kernel,
+        grid=(count // TILE,),
+        in_specs=[rows, fixed, code_spec],
+        out_specs=[rows, few],
+        out_shape=[
+            jax.ShapeDtypeStruct((count, LANES), jnp.float32),
+            jax.ShapeDtypeStruct((count // QLEN, LANES), jnp.float32),
+        ],
+        name="tile_forward",
+    )(queries, passages, codes)
+
+
+def tile_backward(queries, passages, codes, inverse, grad_logits):
+    rows, fixed, code_spec, few = tile_specs(passages.shape[0])
+    count = queries.shape[0]
+    return pl.pallas_call(
+        tile_backward_kernel,
+        grid=(count // TILE,),
+        in_specs=[rows, fixed, code_spec, rows, few],
+        out_specs=[rows, fixed],
+        out_shape=[
+            jax.ShapeDtypeStruct((count, PROJ), jnp.bfloat16),
+            jax.ShapeDtypeStruct(passages.shape, jnp.float32),
+        ],
+        name="tile_backward",
+    )(queries, passages, codes, inverse, grad_logits)
+
+
+def add_low(first, second):
+    return (first.astype(jnp.float32) + second.astype(jnp.float32)).astype(jnp.bfloat16)
+
+
+def halved(part, axes, bit):
+    place = axes.index(bit)
+    mine = (lax.axis_index("pb") >> bit) & 1
+    keep = lax.dynamic_index_in_dim(part, mine, place, False)
+    send = lax.dynamic_index_in_dim(part, 1 - mine, place, False)
+    pairs = [(i, i ^ (1 << bit)) for i in range(lax.axis_size("pb"))]
+    return add_low(keep, lax.ppermute(send, "pb", pairs)), [a for a in axes if a != bit]
+
+
+def scatter_sum(part):
+    wide = lax.axis_size("pb")
+    narrow = lax.axis_size("pa")
+    bits = list(range(wide.bit_length() - 1))
+    rows = part.shape[0] // (wide * narrow)
+    columns = part.shape[1]
+    part = part.reshape((2,) * len(bits) + (narrow, rows, columns))
+    axes = bits[::-1]
+    part, axes = halved(part, axes, 0)
+    cut = columns // 2 // LANES * LANES
+    pieces = [part[..., :cut], part[..., cut:]]
+    orders = [bits[1:], bits[:0:-1]]
+    done = []
+    for piece, order in zip(pieces, orders):
+        left = axes
+        for bit in order:
+            piece, left = halved(piece, left, bit)
+        done.append(piece)
+    joined = jnp.concatenate(done, axis=-1)
+    mine = lax.axis_index("pa")
+    total = lax.dynamic_index_in_dim(joined, mine, 0, False).astype(jnp.float32)
+    for step in range(1, narrow):
+        send = lax.dynamic_index_in_dim(joined, mine ^ step, 0, False)
+        pairs = [(i, i ^ step) for i in range(narrow)]
+        total = total + lax.ppermute(send, "pa", pairs).astype(jnp.float32)
+    return total
 
 
 def body(
@@ -235,39 +288,29 @@
     passage_emb = embedded_low[query_count:]
     usable = (mask_row == 1) & (token_ids[0] >= SKIP_IDS)
     own_codes = jnp.where(usable, bins_row, -1)
-    narrow_count = lax.axis_size("pa")
-    wide_count = lax.axis_size("pb")
-    narrow_index = lax.axis_index("pa")
-    wide_index = lax.axis_index("pb")
-    group_queries = QRY_DEV * narrow_count
-    slot_ids = lax.broadcasted_iota(jnp.int32, (1, PSG_DEV), 1)
-    block_queries = lax.all_gather(query_emb, "pa", axis=0, tiled=True)
-    gathered, gathered_codes = (
-        lax.all_gather(passage_emb, "pb", axis=0, tiled=True),
-        lax.all_gather(own_codes.astype(jnp.bfloat16)[None, :], "pb", axis=0, tiled=True),
-    )
-    passage_tiles = gathered.reshape(wide_count, token_count, PROJ)
-    code_tiles = gathered_codes.astype(jnp.int32)
-    exp_tiles, sum_tiles = passage_tile_sums(block_queries, passage_tiles, code_tiles)
-    tile_logits = query_logits(sum_tiles)
-    logits = jnp.transpose(tile_logits, (1, 0, 2)).reshape(group_queries, wide_count * PSG_DEV)
-    shard_ids = lax.broadcasted_iota(jnp.int32, (wide_count, 1), 0)
-    column_ids = ((shard_ids * narrow_count + narrow_index) * PSG_DEV + slot_ids).reshape(-1)
-    wanted = lax.dynamic_slice_in_dim(positives, wide_index * group_queries, group_queries)
-    stats, positive_hit = local_stats(logits, column_ids, wanted)
-    merged = merged_2(stats, "pa", merge_stats)
-    losses, grad_logits = finish_loss(logits, merged, positive_hit)
-    own_losses = lax.dynamic_slice_in_dim(losses, narrow_index * QRY_DEV, QRY_DEV)
-    grad_tiles = jnp.transpose(grad_logits.reshape(group_queries, wide_count, PSG_DEV), (1, 0, 2))
-    block_grad, passage_grad_tiles = passage_tile_grads(
-        block_queries, passage_tiles, code_tiles, sum_tiles, grad_tiles, exp_tiles
-    )
-    grad_query_emb = lax.psum_scatter(
-        block_grad.astype(jnp.bfloat16), "pa", scatter_dimension=0, tiled=True
+    own_index = lax.axis_index("pb") * lax.axis_size("pa") + lax.axis_index("pa")
+    all_queries = lax.all_gather(query_emb, ("pb", "pa"), axis=0, tiled=True)
+    code_row = own_codes[None, :]
+    inverse, own_logits = tile_forward(all_queries, passage_emb, code_row)
+    gathered = lax.all_gather(own_logits[:, :PSG_DEV], ("pb", "pa"), axis=0)
+    row_peak = jnp.max(gathered, axis=(0, 2))
+    log_norm = row_peak + jnp.log(
+        jnp.sum(jnp.exp(gathered - row_peak[None, :, None]), axis=(0, 2))
+    )
+    shard_ids = lax.broadcasted_iota(jnp.int32, gathered.shape, 0)
+    slot_ids = lax.broadcasted_iota(jnp.int32, gathered.shape, 2)
+    hits = shard_ids * PSG_DEV + slot_ids == positives[None, :, None]
+    losses = log_norm - jnp.sum(jnp.where(hits, gathered, 0.0), axis=(0, 2))
+    queries_here = query_count // QLEN
+    own_losses = lax.dynamic_slice_in_dim(losses, own_index * queries_here, queries_here)
+    own_columns = own_index * PSG_DEV + lax.broadcasted_iota(jnp.int32, own_logits.shape, 1)
+    grad_logits = jnp.exp(own_logits - log_norm[:, None]) - (
+        own_columns == positives[:, None]
     ).astype(jnp.float32)
-    grad_passage_emb = lax.psum_scatter(
-        passage_grad_tiles.reshape(-1, PROJ), "pb", scatter_dimension=0, tiled=True
-    )
+    all_grad, grad_passage_emb = tile_backward(
+        all_queries, passage_emb, code_row, inverse, grad_logits
+    )
+    grad_query_emb = scatter_sum(all_grad)
     grad_embedded = jnp.concatenate([grad_query_emb, grad_passage_emb], axis=0)
     unit_pull = jax.vjp(unit_rows, projected)[1]
     grad_projected = unit_pull(grad_embedded)[0].astype(jnp.bfloat16)
@@ -297,17 +340,36 @@
     grad_united_rows = jnp.concatenate([grad_query_united, grad_passage_united], axis=0)
     grad_united = contract_rows(all_rows, grad_united_rows)
     grad_rows = times_transposed(grad_united_rows, united_weight) + grad_hidden_one
+    rows_in = D // (lax.axis_size("pb") * lax.axis_size("pa"))
+    blocks = D // rows_in
+    vectors = jnp.concatenate(
+        [
+            v.reshape(blocks, rows_in, -1)
+            for v in (
+                grad_first_gain, grad_first_shift, grad_second_gain, grad_second_shift, grad_up_bias
+            )
+        ],
+        axis=-1,
+    ).reshape(D, -1)
+    vectors = jnp.pad(vectors, ((0, 0), (0, LANES - vectors.shape[1])))
+    down_sum = scatter_sum(grad_down)
+    up_sum = scatter_sum(grad_up)
+    mixed = scatter_sum(
+        jnp.concatenate([grad_output, grad_project, vectors.astype(jnp.bfloat16)], axis=1)
+    )
+    united_sum = scatter_sum(grad_united)
+    small = mixed[:, D + PROJ :]
     shared = (
-        lax.psum_scatter(grad_united, ("pb", "pa"), scatter_dimension=0, tiled=True),
-        lax.psum_scatter(grad_output, ("pb", "pa"), scatter_dimension=0, tiled=True),
-        lax.psum_scatter(grad_first_gain, ("pb", "pa"), scatter_dimension=0, tiled=True),
-        lax.psum_scatter(grad_first_shift, ("pb", "pa"), scatter_dimension=0, tiled=True),
-        lax.psum_scatter(grad_up, ("pb", "pa"), scatter_dimension=0, tiled=True),
-        lax.psum_scatter(grad_up_bias, ("pb", "pa"), scatter_dimension=0, tiled=True),
-        lax.psum_scatter(grad_down, ("pb", "pa"), scatter_dimension=0, tiled=True),
-        lax.psum_scatter(grad_second_gain, ("pb", "pa"), scatter_dimension=0, tiled=True),
-        lax.psum_scatter(grad_second_shift, ("pb", "pa"), scatter_dimension=0, tiled=True),
-        lax.psum_scatter(grad_project, ("pb", "pa"), scatter_dimension=0, tiled=True),
+        united_sum,
+        mixed[:, :D],
+        small[:, 0],
+        small[:, 1],
+        up_sum,
+        small[:, 4:8].reshape(-1),
+        down_sum,
+        small[:, 2],
+        small[:, 3],
+        mixed[:, D : D + PROJ],
     )
     return (
         query_emb,

time: 1130 us -> 618 us (0.55)
  waiting for transfers between devices: 548 us -> 59.5 us
  matrix products: 284 us -> 206 us
  blocking collectives: 77.5 us -> 143 us
  local copies, waits for them, and re-layouts: 120 us -> 68.2 us
  starting transfers between devices: 0.33 us -> 38.1 us
  Pallas kernels: 0 us -> 17.1 us
  between operations: 16 us -> 2.09 us
    reduce_scatter x6 -> x0, waiting for transfers between devices: 548 us -> none  [the longest x1 142 us: body(): lax.psum_scatter(grad_down, ('pb', 'pa'), scatter_dimension=0, tiled=True)]
    all_gather x2, blocking collectives: 24.8 us -> 143 us  [the longest x1 79.1 us: body(): all_queries = lax.all_gather(query_emb, ('pb', 'pa'), axis=0, tiled=True)]
    dot_general x40 -> x0, matrix products: 72.5 us -> none  [the longest x8 16.8 us: tile_forward(): jnp.einsum('te,pe->tp', query_part, passage_part, preferred_element_type=...]
    ppermute x0 -> x38, waiting for transfers between devices: none -> 59.5 us  [the longest x23 42.9 us: halved(): lax.ppermute(send, 'pb', pairs)]
    unnamed x2 -> x0, blocking collectives: 52.7 us -> none
    dynamic_slice x34 -> x1, local copies, waits for them, and re-layouts: 48.8 us -> 1.39 us  [body(): lax.dynamic_slice_in_dim(losses, own_index * queries_here, queries_here)]
    ppermute x0 -> x38, starting transfers between devices: none -> 38.1 us  [the longest x15 21.7 us: scatter_sum(): total = total + lax.ppermute(send, 'pa', pairs).astype(jnp.float32)]
    pallas_call x0 -> x2, Pallas kernels: none -> 17.1 us  [the longest x1 9.14 us: tile_backward(): pl.pallas_call(tile_backward_kernel, grid=(count // TILE,), in_specs=[row...]
  transfers between devices with their start and end apart: 8 -> 38, of which waited for: 6 -> 16; matrix products, arithmetic and copies ran while one was open for 8% -> 7% of each run, Pallas kernels for 0% -> 0%
where the time goes in v1:
time: 618 us; the launch traced here: 608 us
  matrix products  206 us (33%)
  blocking collectives  143 us (23%)
  other arithmetic  74.4 us (12%)
  local copies, waits for them, and re-layouts  68.2 us (11%)
  waiting for transfers between devices  59.5 us (10%)
  starting transfers between devices  38.1 us (6%)
  Pallas kernels  17.1 us (3%)
    all_gather x1, blocking collectives, body(): all_queries = lax.all_gather(query_emb, ('pb', 'pa'), axis=0, tiled=True)  79.1 us
    all_gather x1, blocking collectives, body(): gathered = lax.all_gather(own_logits[:, :PSG_DEV], ('pb', 'pa'), axis=0)  64.1 us
    ppermute x23, waiting for transfers between devices, halved(): lax.ppermute(send, 'pb', pairs)  42.9 us
    dot_general x5, matrix products, times_transposed(): jnp.einsum('re,de->rd', operand, partner, preferred_element_type=jnp.floa...  34.4 us
    dot_general x1, matrix products, body(): jnp.dot(norm_one_low, up_weight, preferred_element_type=jnp.float32)  29.6 us
    dot_general x5, matrix products, contract_rows(): jnp.einsum('rd,re->de', operand, partner, preferred_element_type=jnp.floa...  26.7 us
    dot_general x2, matrix products, attend_backward(): jnp.einsum('qhd,khd->hqk', grad_heads, head_value, preferred_element_type...  25.5 us
    convert_element_type x2, other arithmetic, attend_backward(): grad_scores = (soft_weights * (grad_weights - centre)).astype(jnp.bfloat16)  24.6 us
  transfers between devices with their start and end apart: 38, of which 16 were waited for; matrix products, arithmetic and copies ran while one was open for 7% of the time, Pallas kernels for 0%

profile of v1, /device:TPU:0, one launch (start us, length us, event | category | flops | bytes accessed | tf_op | source)
XLA Modules:
  0.0 608.4 jit_solution(6374359049320813090)
XLA Ops:
  4.5 3.3 convolution_convert_fusion
  8.6 2.0 slice.138
  10.6 5.8 copy.94
  16.4 2.3 reshape.391
  18.7 2.0 fusion.126
  20.7 1.8 copy.137
  25.9 13.1 %fusion = (f32[12,768]{1,0:T(8,128)S(1)}, f32[12,768,768]{1,2,0:T(8,128)}) fusion(pred[768,768]{0,1:T(8,128)(4,1)S(1)} %fusion.14, bf16[768,3,12,64]{0,3,2,1:T(8,128)(2,1)} %bitcast.289), kind=kOutput, calls=%fused_computation.5 | convolution fusion | flops 927194112 | bytes 31297536 | tf_op jit(solution)/shard_map/qhd,khd->hqk/dot_general | solution.py:58
  39.0 12.6 %exponential_reduce_fusion = f32[12,768]{1,0:T(8,128)S(1)} fusion(f32[12,768,768]{1,2,0:T(8,128)} %get-tuple-element.72, f32[12,768]{1,0:T(8,128)S(1)} %get-tuple-element.71, pred[768,768]{0,1:T(8,128)(4,1)S(1)} %fusion.14), kind=kLoop, calls=%fused_computation.3 | loop fusion | flops 28302336 | bytes 28975104 | tf_op jit(solution)/shard_map/reduce_sum | solution.py:68
  51.7 23.6 %convolution_convert_fusion.7 = bf16[12,64,768]{2,1,0:T(8,128)(2,1)S(1)} fusion(bf16[768,3,12,64]{0,3,2,1:T(8,128)(2,1)} %bitcast.290, f32[12,768,768]{1,2,0:T(8,128)} %get-tuple-element.72, f32[12,768]{1,0:T(8,128)S(1)} %log_add_fusion, pred[768,768]{0,1:T(8,128)(4,1)S(1)} %fusion.14), kind=kOutput, calls=%fused_computation.70 | convolution fusion | flops 934871040 | bytes 31297536 | tf_op jit(solution)/shard_map/hqk,khd->qhd/dot_general | solution.py:70
  75.6 1.8 fusion.128
  78.9 29.6 %multiply_convert_fusion.1 = (bf16[832,3072]{1,0:T(8,128)(2,1)S(1)}, f32[832,3072]{1,0:T(8,128)}, f32[832,3072]{1,0:T(8,128)}) fusion(f32[3072]{0:T(1024)S(1)} %copy-done.64, bf16[768,3072]{1,0:T(8,128)(2,1)} %param.26, f32[832,768]{1,0:T(8,128)S(1)} %get-tuple-element.76, f32[768]{0:T(1024)S(1)} %copy-done.66, f32[768]{0:T(1024)S(1)} %copy-done.53, ...), kind=kOutput, calls=%fused_computation.10 | convolution fusion | flops 4097753088 | bytes 32858624 | tf_op jit(solution)/shard_map/dot_general | solution.py:279
  108.6 4.4 fusion.129
  118.5 79.1 %all_gather.9.query_ref = bf16[2048,128]{1,0:T(8,128)(2,1)} all-gather(bf16[64,128]{1,0:T(8,128)(2,1)} %slice.142), channel_id=1, replica_groups=mesh['pb'=8,'pa'=4] {'pb','pa'}, dimensions={0}, use_global_device_ids=true | all-gather | bytes 540672 | tf_op jit(solution)/shard_map/all_gather | solution.py:292
  197.6 7.9 %tile_forward.1 = (f32[2048,128]{1,0:T(8,128)}, f32[64,128]{1,0:T(8,128)}) custom-call(bf16[2048,128]{1,0:T(8,128)(2,1)} %all_gather.9.query_ref, bf16[768,128]{1,0:T(8,128)(2,1)} %slice.143.passage_ref, s32[1,768]{1,0:T(1,128)} %get-tuple-element.69.code_ref), custom_call_target="tpu_custom_call" | custom-call | tf_op jit(solution)/shard_map/tile_forward/pallas_call | solution.py:167
  208.3 64.1 %all-gather.1 = f32[32,64,4]{1,2,0:T(4,128)S(1)} all-gather(f32[1,64,4]{1,2,0:T(4,128)} %copy.96), channel_id=2, replica_groups=mesh['pb'=8,'pa'=4] {'pb','pa'}, dimensions={0}, use_global_device_ids=true | all-gather | bytes 33792 | tf_op jit(solution)/shard_map/all_gather | solution.py:295
  277.5 9.1 %tile_backward.1 = (bf16[2048,128]{1,0:T(8,128)(2,1)}, f32[768,128]{1,0:T(8,128)}) custom-call(bf16[2048,128]{1,0:T(8,128)(2,1)} %all_gather.9.query_ref, bf16[768,128]{1,0:T(8,128)(2,1)} %slice.143.passage_ref, s32[1,768]{1,0:T(1,128)} %get-tuple-element.69.code_ref, f32[2048,128]{1,0:T(8,128)} %get-tuple-element.20.inverse_ref, ...), custom_call_target="tpu_custom_call" | custom-call | tf_op jit(solution)/shard_map/tile_backward/pallas_call | solution.py:183
  286.6 1.7 dynamic-slice_bitcast_fusion.14
  288.3 1.9 collective-permute-done
  293.1 5.3 collective-permute-done.1
  300.8 4.6 collective-permute-done.2
  307.5 2.2 collective-permute-start.3
  312.6 3.0 collective-permute-done.5
  319.8 2.4 convolution_convert_fusion.8
  325.1 7.2 %convolution_convert_fusion.1 = bf16[3072,768]{1,0:T(8,128)(2,1)} fusion(bf16[832,3072]{1,0:T(8,128)(2,1)S(1)} %bitcast.323, f32[832,768]{1,0:T(8,128)S(1)} %get-tuple-element.38, f32[832]{0:T(1024)S(1)} %negate_multiply_fusion.2), kind=kOutput, calls=%fused_computation.25 | convolution fusion | flops 3929505792 | bytes 12389632 | tf_op jit(solution)/shard_map/rd,re->de/dot_general | solution.py:43
  332.3 16.7 %fusion.130 = (bf16[3072]{0:T(1024)(128)(2,1)}, bf16[832,3072]{1,0:T(8,128)(2,1)}) fusion(f32[832,3072]{1,0:T(8,128)} %get-tuple-element.42, bf16[3072,768]{1,0:T(8,128)(2,1)} %param.28, f32[832,768]{1,0:T(8,128)} %copy-done.18, f32[832]{0:T(1024)S(1)} %negate_multiply_fusion.2, f32[832,3072]{1,0:T(8,128)} %get-tuple-element.77, f32[3072]{0:T(1024)S(1)} %copy-done.65), kind=kOutput, calls=%fused_computation.311 | convolution fusion | flops 3968037888 | bytes 32855296 | tf_op jit(solution)/shard_map/re,de->rd/dot_general | solution.py:48
  349.0 10.2 %multiply_reduce_fusion.2 = (bf16[768]{0:T(1024)(128)(2,1)}, f32[832]{0:T(1024)S(1)}, bf16[768]{0:T(1024)(128)(2,1)}, f32[832,768]{1,0:T(8,128)S(1)}) fusion(f32[832,768]{1,0:T(8,128)S(1)} %copy-done.7, f32[832]{0:T(1024)S(1)} %copy-done.44, f32[832]{0:T(1024)S(1)} %broadcast_multiply_fusion.1, f32[768]{0:T(1024)S(1)} %copy-done.54, ...), kind=kOutput, calls=%fused_computation.42 | convolution fusion | flops 3932256000 | bytes 17517568 | tf_op jit(solution)/shard_map/re,de->rd/dot_general | solution.py:48
  359.2 7.7 %convolution_convert_fusion.2 = bf16[768,3072]{1,0:T(8,128)(2,1)} fusion(bf16[832,3072]{1,0:T(8,128)(2,1)S(1)} %copy-done.70, f32[832,768]{1,0:T(8,128)S(1)} %copy-done.7, f32[768]{0:T(1024)S(1)} %copy-done.67, f32[768]{0:T(1024)S(1)} %copy-done.54, f32[832]{0:T(1024)S(1)} %copy-done.44, f32[832]{0:T(1024)S(1)} %broadcast_multiply_fusion.1), kind=kOutput, calls=%fused_computation.26 | convolution fusion | flops 3931422720 | bytes 12399104 | tf_op jit(solution)/shard_map/rd,re->de/dot_general | solution.py:43
  368.3 2.7 convolution_convert_fusion.5
  374.1 1.7 copy.147
  375.8 2.1 fusion.29
  382.3 2.4 copy.110
  384.7 17.8 %fusion.19 = bf16[768,1,12,64]{0,3,2,1:T(8,128)(2,1)} fusion(bf16[768,12,64]{0,2,1:T(8,128)(2,1)} %bitcast.304, f32[12,768,768]{1,2,0:T(8,128)} %get-tuple-element.72, f32[12,768]{1,0:T(8,128)} %copy-done.29, pred[768,768]{0,1:T(8,128)(4,1)} %copy-done.3), kind=kOutput, calls=%fused_computation.71 | convolution fusion | flops 934871040 | bytes 31297536 | tf_op jit(solution)/shard_map/hqk,qhd->khd/dot_general | solution.py:92
  402.5 24.1 %multiply_reduce_fusion = (f32[12,768]{1,0:T(8,128)}, f32[12,768,768]{1,2,0:T(8,128)}) fusion(f32[12,768,768]{1,2,0:T(8,128)} %get-tuple-element.72, f32[12,768]{1,0:T(8,128)S(1)} %copy-done.30, pred[768,768]{0,1:T(8,128)(4,1)S(1)} %copy-done.4, bf16[768,12,64]{0,2,1:T(8,128)(2,1)S(1)} %bitcast.305, bf16[768,3,12,64]{0,3,2,1:T(8,128)(2,1)} %bitcast.291), kind=kOutput, calls=%fused_computation.1 | convolution fusion | flops 941349888 | bytes 59645952 | tf_op jit(solution)/shard_map/qhd,khd->hqk/dot_general | solution.py:79
  426.5 23.5 %multiply_convert_fusion = bf16[12,768,768]{1,2,0:T(8,128)(2,1)} fusion(f32[12,768,768]{1,2,0:T(8,128)} %get-tuple-element.85, f32[12,768,768]{1,2,0:T(8,128)} %get-tuple-element.72, f32[12,768]{1,0:T(8,128)} %get-tuple-element.84, f32[12,768]{1,0:T(8,128)} %copy-done.29, pred[768,768]{0,1:T(8,128)(4,1)} %copy-done.3), kind=kLoop, calls=%fused_computation | loop fusion | flops 42467328 | bytes 71442432 | tf_op jit(solution)/shard_map/convert_element_type | solution.py:83
  450.0 10.8 %fusion.21 = bf16[768,1,12,64]{0,3,2,1:T(8,128)(2,1)} fusion(bf16[12,768,768]{1,2,0:T(8,128)(2,1)} %multiply_convert_fusion, bf16[768,3,12,64]{0,3,2,1:T(8,128)(2,1)} %bitcast.292), kind=kOutput, calls=%fused_computation.73 | convolution fusion | flops 907149312 | bytes 16515072 | tf_op jit(solution)/shard_map/hqk,qhd->khd/dot_general | solution.py:89
  460.8 9.0 %fusion.20 = bf16[768,1,12,64]{0,3,2,1:T(8,128)(2,1)} fusion(bf16[12,768,768]{1,2,0:T(8,128)(2,1)} %multiply_convert_fusion, bf16[768,3,12,64]{0,3,2,1:T(8,128)(2,1)} %bitcast.293), kind=kOutput, calls=%fused_computation.72 | convolution fusion | flops 907149312 | bytes 16515072 | tf_op jit(solution)/shard_map/hqk,khd->qhd/dot_general | solution.py:85
  472.7 1.6 copy.116
  475.1 2.6 fusion.17
  477.8 2.6 copy.117
  480.4 2.1 dynamic-slice_bitcast_fusion.3
  482.4 2.1 pad_maximum_fusion.9
  484.5 2.1 copy.135
  486.6 3.4 dynamic-slice_bitcast_fusion.1
  491.5 6.7 %convolution_convert_fusion.3 = bf16[768,2304]{1,0:T(8,128)(2,1)S(1)} fusion(bf16[832,768]{1,0:T(8,128)(2,1)S(1)} %copy-done.50, bf16[768,2304]{0,1:T(8,128)(2,1)S(1)} %bitcast.306, bf16[64,2304]{0,1:T(8,128)(2,1)S(1)} %bitcast.312), kind=kOutput, calls=%fused_computation.27 | convolution fusion | flops 2953838592 | bytes 8650752 | tf_op jit(solution)/shard_map/rd,re->de/dot_general | solution.py:43
  499.9 4.7 add_add_fusion.2
  511.3 2.3 collective-permute-done.15
  514.3 4.2 collective-permute-done.17
  518.6 2.0 collective-permute-start.18
  520.7 2.6 collective-permute-done.18
  524.2 2.8 collective-permute-start.20
  531.2 2.0 collective-permute-start.7
  535.2 1.6 slice_reduce_fusion
  538.4 2.4 collective-permute-done.7
  542.7 6.0 collective-permute-done.9
  550.2 3.1 fusion.8
  555.6 2.6 fusion.9
  558.8 3.0 collective-permute-start.12
  566.2 2.1 collective-permute-done.13
  572.2 10.4 %collective-permute-done.23 = bf16[2,4,24,1536]{3,2,1,0:T(8,128)(2,1)S(1)} collective-permute-done((bf16[2,4,24,1536]{3,2,1,0:T(8,128)(2,1)S(1)}, bf16[2,4,24,1536]{3,2,1,0:T(8,128)(2,1)S(1)}, u32[]{:S(2)}, u32[]{:S(2)}) %collective-permute-start.23) | collective-permute-done | bytes 589856 | tf_op jit(solution)/shard_map/ppermute | solution.py:206
  584.8 2.2 collective-permute-done.32
  587.4 3.0 collective-permute-start.36
  592.1 3.0 collective-permute-start.28
  596.7 7.5 %collective-permute-done.36 = bf16[96,768]{1,0:T(8,128)(2,1)S(1)} collective-permute-done((bf16[96,768]{1,0:T(8,128)(2,1)S(1)}, bf16[96,768]{1,0:T(8,128)(2,1)S(1)}, u32[]{:S(2)}, u32[]{:S(2)}) %collective-permute-start.36) | collective-permute-done | bytes 147488 | tf_op jit(solution)/shard_map/ppermute | solution.py:233
  605.0 2.4 collective-permute-done.28
  (339 shorter events, 93.4 us)
Async XLA Ops:
  24.7 50.6 %copy-start.8 = (f32[12,64,64]{1,2,0:T(8,128)}, f32[12,64,64]{1,2,0:T(8,128)S(1)}, u32[]{:S(2)}) copy-start(f32[12,64,64]{1,2,0:T(8,128)S(1)} %get-tuple-element.74) | copy-start | bytes 589828
  24.8 50.5 %copy-start.32 = (f32[12,64]{1,0:T(8,128)}, f32[12,64]{1,0:T(8,128)S(1)}, u32[]{:S(2)}) copy-start(f32[12,64]{1,0:T(8,128)S(1)} %log_add_fusion.1) | copy-start | bytes 9220
  25.9 25.8 %copy-start.3 = (pred[768,768]{0,1:T(8,128)(4,1)}, pred[768,768]{0,1:T(8,128)(4,1)S(1)}, u32[]{:S(2)}) copy-start(pred[768,768]{0,1:T(8,128)(4,1)S(1)} %fusion.14) | copy-start | bytes 1769476
  51.7 23.6 %copy-start.29 = (f32[12,768]{1,0:T(8,128)}, f32[12,768]{1,0:T(8,128)S(1)}, u32[]{:S(2)}) copy-start(f32[12,768]{1,0:T(8,128)S(1)} %log_add_fusion) | copy-start | bytes 110596
  51.7 23.6 %copy-start.19 = (bf16[64,1,12,64]{0,3,2,1:T(8,128)(2,1)S(1)}, bf16[64,1,12,64]{0,3,2,1:T(8,128)(2,1)}, u32[]{:S(2)}) copy-start(bf16[64,1,12,64]{0,3,2,1:T(8,128)(2,1)} %copy.137) | copy-start | bytes 294916
  51.7 23.9 %copy-start.49 = (bf16[832,768]{1,0:T(8,128)(2,1)S(1)}, bf16[832,768]{1,0:T(8,128)(2,1)}, u32[]{:S(2)}) copy-start(bf16[832,768]{1,0:T(8,128)(2,1)} %copy-done.48) | copy-start | bytes 3833860
  51.7 23.9 %copy-start.62 = (bf16[768,768]{1,0:T(8,128)(2,1)S(1)}, bf16[768,768]{1,0:T(8,128)(2,1)}, u32[]{:S(2)}) copy-start(bf16[768,768]{1,0:T(8,128)(2,1)} %param.23) | copy-start | bytes 3538948
  75.6 32.9 %slice-start.4 = ((s8[4718592]{0:T(1024)(128)(4,1)}), s8[524288]{0:T(1024)(128)(4,1)S(1)}, s32[]{:S(2)}) async-start(s8[4718592]{0:T(1024)(128)(4,1)} %bitcast.318), calls=%async_computation.4 | async-start | bytes 1048576
  77.4 31.1 %copy-start.6 = (f32[832,768]{1,0:T(8,128)}, f32[832,768]{1,0:T(8,128)S(1)}, u32[]{:S(2)}) copy-start(f32[832,768]{1,0:T(8,128)S(1)} %get-tuple-element.76) | copy-start | bytes 7667716
  78.8 29.7 %copy-start.43 = (f32[832]{0:T(1024)}, f32[832]{0:T(1024)S(1)}, u32[]{:S(2)}) copy-start(f32[832]{0:T(1024)S(1)} %fusion.104) | copy-start | bytes 9988
  78.9 29.7 %slice-start.5 = ((s8[4718592]{0:T(1024)(128)(4,1)}), s8[4194304]{0:T(1024)(128)(4,1)S(1)}, s32[]{:S(2)}) async-start(s8[4718592]{0:T(1024)(128)(4,1)} %bitcast.318), calls=%async_computation.5 | async-start | bytes 8388608
  288.3 1.9 collective-permute-start
  292.6 5.9 collective-permute-start.1
  300.8 4.6 collective-permute-start.2
  307.5 5.1 collective-permute-start.3
  309.7 5.9 collective-permute-start.5
  309.7 5.9 collective-permute-start.4
  311.2 11.0 %copy-start.2 = (f32[832,768]{1,0:T(8,128)S(1)}, f32[832,768]{1,0:T(8,128)}, u32[]{:S(2)}) copy-start(f32[832,768]{1,0:T(8,128)} %copy-done.1) | copy-start | bytes 7667716
  311.2 11.0 %copy-start.25 = (bf16[768,128]{1,0:T(8,128)(2,1)S(1)}, bf16[768,128]{1,0:T(8,128)(2,1)}, u32[]{:S(2)}) copy-start(bf16[768,128]{1,0:T(8,128)(2,1)} %param.31) | copy-start | bytes 589828
  332.3 16.7 %copy-start.7 = (f32[832,768]{1,0:T(8,128)S(1)}, f32[832,768]{1,0:T(8,128)}, u32[]{:S(2)}) copy-start(f32[832,768]{1,0:T(8,128)} %copy-done.6) | copy-start | bytes 7667716
  332.3 16.7 %copy-start.44 = (f32[832]{0:T(1024)S(1)}, f32[832]{0:T(1024)}, u32[]{:S(2)}) copy-start(f32[832]{0:T(1024)} %copy-done.43) | copy-start | bytes 9988
  332.3 16.7 %copy-start.54 = (f32[768]{0:T(1024)S(1)}, f32[768]{0:T(1024)}, u32[]{:S(2)}) copy-start(f32[768]{0:T(1024)} %param.24) | copy-start | bytes 9220
  349.0 10.2 %copy-start.67 = (f32[768]{0:T(1024)S(1)}, f32[768]{0:T(1024)}, u32[]{:S(2)}) copy-start(f32[768]{0:T(1024)} %param.25) | copy-start | bytes 9220
  349.0 10.2 %copy-start.70 = (bf16[832,3072]{1,0:T(8,128)(2,1)S(1)}, bf16[832,3072]{1,0:T(8,128)(2,1)}, u32[]{:S(2)}) copy-start(bf16[832,3072]{1,0:T(8,128)(2,1)} %get-tuple-element.89) | copy-start | bytes 15335428
  384.7 17.8 %copy-start.4 = (pred[768,768]{0,1:T(8,128)(4,1)S(1)}, pred[768,768]{0,1:T(8,128)(4,1)}, u32[]{:S(2)}) copy-start(pred[768,768]{0,1:T(8,128)(4,1)} %copy-done.3) | copy-start | bytes 1769476
  384.7 17.8 %copy-start.13 = (bf16[768,768]{0,1:T(8,128)(2,1)S(1)}, bf16[768,768]{0,1:T(8,128)(2,1)}, u32[]{:S(2)}) copy-start(bf16[768,768]{0,1:T(8,128)(2,1)} %copy.110) | copy-start | bytes 3538948
  384.7 17.8 %copy-start.30 = (f32[12,768]{1,0:T(8,128)S(1)}, f32[12,768]{1,0:T(8,128)}, u32[]{:S(2)}) copy-start(f32[12,768]{1,0:T(8,128)} %copy-done.29) | copy-start | bytes 110596
  460.8 9.6 %copy-start.61 = (bf16[768]{0:T(1024)(128)(2,1)S(1)}, bf16[768]{0:T(1024)(128)(2,1)}, u32[]{:S(2)}) copy-start(bf16[768]{0:T(1024)(128)(2,1)} %get-tuple-element.25) | copy-start | bytes 4612
  460.8 10.2 %copy-start.60 = (bf16[768]{0:T(1024)(128)(2,1)S(1)}, bf16[768]{0:T(1024)(128)(2,1)}, u32[]{:S(2)}) copy-start(bf16[768]{0:T(1024)(128)(2,1)} %get-tuple-element.28) | copy-start | bytes 4612
  460.8 10.8 %copy-start.51 = (bf16[3072]{0:T(1024)(128)(2,1)S(1)}, bf16[3072]{0:T(1024)(128)(2,1)}, u32[]{:S(2)}) copy-start(bf16[3072]{0:T(1024)(128)(2,1)} %get-tuple-element.88) | copy-start | bytes 18436
  482.4 22.2 %collective-permute-start.14 = (bf16[2,2,4,24,1024]{4,3,2,1,0:T(8,128)(2,1)}, bf16[2,2,4,24,1024]{4,3,2,1,0:T(8,128)(2,1)}, u32[]{:S(2)}, u32[]{:S(2)}) collective-permute-start(bf16[2,2,4,24,1024]{4,3,2,1,0:T(8,128)(2,1)} %dynamic-slice_bitcast_fusion.3), channel_id=1, source_target_pairs={{0,4},{4,0},{8,12},{12,8},{16,20},{20,16},{24,28},{28,24},{1,5},{5... | collective-permute-start | bytes 2359304 | tf_op jit(solution)/shard_map/ppermute | solution.py:206
  491.5 14.8 %slice-start.2 = ((s8[4718592]{0:T(1024)(128)(4,1)}), s8[4194304]{0:T(1024)(128)(4,1)S(1)}, s32[]{:S(2)}) async-start(s8[4718592]{0:T(1024)(128)(4,1)} %bitcast.301), calls=%async_computation.2 | async-start | bytes 8388608
  498.4 28.5 %collective-permute-start.6 = (bf16[2,2,4,24,2304]{4,3,2,1,0:T(8,128)(2,1)S(1)}, bf16[2,2,4,24,2304]{4,3,2,1,0:T(8,128)(2,1)S(1)}, u32[]{:S(2)}, u32[]{:S(2)}) collective-permute-start(bf16[2,2,4,24,2304]{4,3,2,1,0:T(8,128)(2,1)S(1)} %dynamic-slice_bitcast_fusion.2), channel_id=1, source_target_pairs={{0,4},{4,0},{8,12},{12,8},{16,20},{20,16},{24,28},{28,24},{1,5},{5... | collective-permute-start | bytes 5308424 | tf_op jit(solution)/shard_map/ppermute | solution.py:206
  506.2 7.4 %collective-permute-start.15 = (bf16[2,4,24,512]{3,2,1,0:T(8,128)(2,1)S(1)}, bf16[2,4,24,512]{3,2,1,0:T(8,128)(2,1)S(1)}, u32[]{:S(2)}, u32[]{:S(2)}) collective-permute-start(bf16[2,4,24,512]{3,2,1,0:T(8,128)(2,1)S(1)} %dynamic-slice_bitcast_fusion.18), channel_id=1, source_target_pairs={{0,8},{4,12},{8,0},{12,4},{16,24},{20,28},{24,16},{28,20},{1,9},{5... | collective-permute-start | bytes 589832 | tf_op jit(solution)/shard_map/ppermute | solution.py:206
  510.2 40.0 %collective-permute-start.30 = (bf16[2,2,4,96,768]{4,3,2,1,0:T(8,128)(2,1)}, bf16[2,2,4,96,768]{4,3,2,1,0:T(8,128)(2,1)}, u32[]{:S(2)}, u32[]{:S(2)}) collective-permute-start(bf16[2,2,4,96,768]{4,3,2,1,0:T(8,128)(2,1)} %dynamic-slice_bitcast_fusion), channel_id=1, source_target_pairs={{0,4},{4,0},{8,12},{12,8},{16,20},{20,16},{24,28},{28,24},{1,5},{5... | collective-permute-start | bytes 7077896 | tf_op jit(solution)/shard_map/ppermute | solution.py:206
  510.7 44.9 %collective-permute-start.22 = (bf16[2,2,4,24,3072]{4,3,2,1,0:T(8,128)(2,1)}, bf16[2,2,4,24,3072]{4,3,2,1,0:T(8,128)(2,1)}, u32[]{:S(2)}, u32[]{:S(2)}) collective-permute-start(bf16[2,2,4,24,3072]{4,3,2,1,0:T(8,128)(2,1)} %dynamic-slice_bitcast_fusion.1), channel_id=1, source_target_pairs={{0,4},{4,0},{8,12},{12,8},{16,20},{20,16},{24,28},{28,24},{1,5},{5... | collective-permute-start | bytes 7077896 | tf_op jit(solution)/shard_map/ppermute | solution.py:206
  510.7 7.8 %collective-permute-start.17 = (bf16[2,4,24,512]{3,2,1,0:T(8,128)(2,1)S(1)}, bf16[2,4,24,512]{3,2,1,0:T(8,128)(2,1)S(1)}, u32[]{:S(2)}, u32[]{:S(2)}) collective-permute-start(bf16[2,4,24,512]{3,2,1,0:T(8,128)(2,1)S(1)} %dynamic-slice_bitcast_fusion.17), channel_id=1, source_target_pairs={{0,16},{4,20},{8,24},{12,28},{16,0},{20,4},{24,8},{28,12},{1,17},{... | collective-permute-start | bytes 589832 | tf_op jit(solution)/shard_map/ppermute | solution.py:206
  513.7 7.0 %collective-permute-start.16 = (bf16[4,24,512]{2,1,0:T(8,128)(2,1)S(1)}, bf16[4,24,512]{2,1,0:T(8,128)(2,1)S(1)}, u32[]{:S(2)}, u32[]{:S(2)}) collective-permute-start(bf16[4,24,512]{2,1,0:T(8,128)(2,1)S(1)} %dynamic-slice_bitcast_fusion.21), channel_id=1, source_target_pairs={{0,16},{4,20},{8,24},{12,28},{16,0},{20,4},{24,8},{28,12},{1,17},{... | collective-permute-start | bytes 294920 | tf_op jit(solution)/shard_map/ppermute | solution.py:206
  518.6 4.7 collective-permute-start.18
  523.4 7.8 %collective-permute-start.19 = (bf16[24,1024]{1,0:T(8,128)(2,1)S(1)}, bf16[24,1024]{1,0:T(8,128)(2,1)S(1)}, u32[]{:S(2)}, u32[]{:S(2)}) collective-permute-start(bf16[24,1024]{1,0:T(8,128)(2,1)S(1)} %get-tuple-element.63), channel_id=1, source_target_pairs={{0,1},{1,0},{2,3},{3,2},{4,5},{5,4},{6,7},{7,6},{8,9},{9,8},{10,11... | collective-permute-start | bytes 147464 | tf_op jit(solution)/shard_map/ppermute | solution.py:233
  524.2 9.0 %collective-permute-start.20 = (bf16[24,1024]{1,0:T(8,128)(2,1)S(1)}, bf16[24,1024]{1,0:T(8,128)(2,1)S(1)}, u32[]{:S(2)}, u32[]{:S(2)}) collective-permute-start(bf16[24,1024]{1,0:T(8,128)(2,1)S(1)} %get-tuple-element.64), channel_id=1, source_target_pairs={{0,2},{1,3},{2,0},{3,1},{4,6},{5,7},{6,4},{7,5},{8,10},{9,11},{10,... | collective-permute-start | bytes 147464 | tf_op jit(solution)/shard_map/ppermute | solution.py:233
  526.9 6.3 %collective-permute-start.21 = (bf16[24,1024]{1,0:T(8,128)(2,1)S(1)}, bf16[24,1024]{1,0:T(8,128)(2,1)S(1)}, u32[]{:S(2)}, u32[]{:S(2)}) collective-permute-start(bf16[24,1024]{1,0:T(8,128)(2,1)S(1)} %get-tuple-element.65), channel_id=1, source_target_pairs={{0,3},{1,2},{2,1},{3,0},{4,7},{5,6},{6,5},{7,4},{8,11},{9,10},{10,... | collective-permute-start | bytes 147464 | tf_op jit(solution)/shard_map/ppermute | solution.py:233
  531.2 9.6 %collective-permute-start.7 = (bf16[2,4,24,1152]{3,2,1,0:T(8,128)(2,1)}, bf16[2,4,24,1152]{3,2,1,0:T(8,128)(2,1)}, u32[]{:S(2)}, u32[]{:S(2)}) collective-permute-start(bf16[2,4,24,1152]{3,2,1,0:T(8,128)(2,1)} %dynamic-slice_bitcast_fusion.9), channel_id=1, source_target_pairs={{0,8},{4,12},{8,0},{12,4},{16,24},{20,28},{24,16},{28,20},{1,9},{5... | collective-permute-start | bytes 1327112 | tf_op jit(solution)/shard_map/ppermute | solution.py:206
  535.2 13.6 %copy-start.14 = (bf16[2,2,4,24,1152]{4,3,2,1,0:T(8,128)(2,1)S(1)}, bf16[2,2,4,24,1152]{4,3,2,1,0:T(8,128)(2,1)}, u32[]{:S(2)}) copy-start(bf16[2,2,4,24,1152]{4,3,2,1,0:T(8,128)(2,1)} %get-tuple-element.47) | copy-start | bytes 2654212
  537.8 10.9 %collective-permute-start.9 = (bf16[2,4,24,1152]{3,2,1,0:T(8,128)(2,1)S(1)}, bf16[2,4,24,1152]{3,2,1,0:T(8,128)(2,1)S(1)}, u32[]{:S(2)}, u32[]{:S(2)}) collective-permute-start(bf16[2,4,24,1152]{3,2,1,0:T(8,128)(2,1)S(1)} %dynamic-slice_bitcast_fusion.8), channel_id=1, source_target_pairs={{0,16},{4,20},{8,24},{12,28},{16,0},{20,4},{24,8},{28,12},{1,17},{... | collective-permute-start | bytes 1327112 | tf_op jit(solution)/shard_map/ppermute | solution.py:206
  542.1 16.4 %collective-permute-start.8 = (bf16[4,24,1152]{2,1,0:T(8,128)(2,1)S(1)}, bf16[4,24,1152]{2,1,0:T(8,128)(2,1)S(1)}, u32[]{:S(2)}, u32[]{:S(2)}) collective-permute-start(bf16[4,24,1152]{2,1,0:T(8,128)(2,1)S(1)} %dynamic-slice_bitcast_fusion.16), channel_id=1, source_target_pairs={{0,16},{4,20},{8,24},{12,28},{16,0},{20,4},{24,8},{28,12},{1,17},{... | collective-permute-start | bytes 663560 | tf_op jit(solution)/shard_map/ppermute | solution.py:206
  548.9 9.7 %collective-permute-start.10 = (bf16[4,24,1152]{2,1,0:T(8,128)(2,1)S(1)}, bf16[4,24,1152]{2,1,0:T(8,128)(2,1)S(1)}, u32[]{:S(2)}, u32[]{:S(2)}) collective-permute-start(bf16[4,24,1152]{2,1,0:T(8,128)(2,1)S(1)} %dynamic-slice_bitcast_fusion.15), channel_id=1, source_target_pairs={{0,8},{4,12},{8,0},{12,4},{16,24},{20,28},{24,16},{28,20},{1,9},{5... | collective-permute-start | bytes 663560 | tf_op jit(solution)/shard_map/ppermute | solution.py:206
  553.7 16.3 %collective-permute-start.31 = (bf16[2,4,96,384]{3,2,1,0:T(8,128)(2,1)S(1)}, bf16[2,4,96,384]{3,2,1,0:T(8,128)(2,1)S(1)}, u32[]{:S(2)}, u32[]{:S(2)}) collective-permute-start(bf16[2,4,96,384]{3,2,1,0:T(8,128)(2,1)S(1)} %dynamic-slice_bitcast_fusion.5), channel_id=1, source_target_pairs={{0,8},{4,12},{8,0},{12,4},{16,24},{20,28},{24,16},{28,20},{1,9},{5... | collective-permute-start | bytes 1769480 | tf_op jit(solution)/shard_map/ppermute | solution.py:206
  555.0 15.9 %collective-permute-start.33 = (bf16[2,4,96,384]{3,2,1,0:T(8,128)(2,1)S(1)}, bf16[2,4,96,384]{3,2,1,0:T(8,128)(2,1)S(1)}, u32[]{:S(2)}, u32[]{:S(2)}) collective-permute-start(bf16[2,4,96,384]{3,2,1,0:T(8,128)(2,1)S(1)} %dynamic-slice_bitcast_fusion.4), channel_id=1, source_target_pairs={{0,16},{4,20},{8,24},{12,28},{16,0},{20,4},{24,8},{28,12},{1,17},{... | collective-permute-start | bytes 1769480 | tf_op jit(solution)/shard_map/ppermute | solution.py:206
  558.7 6.0 collective-permute-start.11
  558.8 5.9 collective-permute-start.12
  561.8 6.5 %collective-permute-start.13 = (bf16[24,2304]{1,0:T(8,128)(2,1)S(1)}, bf16[24,2304]{1,0:T(8,128)(2,1)S(1)}, u32[]{:S(2)}, u32[]{:S(2)}) collective-permute-start(bf16[24,2304]{1,0:T(8,128)(2,1)S(1)} %get-tuple-element.62), channel_id=1, source_target_pairs={{0,3},{1,2},{2,1},{3,0},{4,7},{5,6},{6,5},{7,4},{8,11},{9,10},{10,... | collective-permute-start | bytes 331784 | tf_op jit(solution)/shard_map/ppermute | solution.py:233
  564.7 17.9 %collective-permute-start.23 = (bf16[2,4,24,1536]{3,2,1,0:T(8,128)(2,1)S(1)}, bf16[2,4,24,1536]{3,2,1,0:T(8,128)(2,1)S(1)}, u32[]{:S(2)}, u32[]{:S(2)}) collective-permute-start(bf16[2,4,24,1536]{3,2,1,0:T(8,128)(2,1)S(1)} %dynamic-slice_bitcast_fusion.7), channel_id=1, source_target_pairs={{0,8},{4,12},{8,0},{12,4},{16,24},{20,28},{24,16},{28,20},{1,9},{5... | collective-permute-start | bytes 1769480 | tf_op jit(solution)/shard_map/ppermute | solution.py:206
  564.7 18.4 %collective-permute-start.25 = (bf16[2,4,24,1536]{3,2,1,0:T(8,128)(2,1)S(1)}, bf16[2,4,24,1536]{3,2,1,0:T(8,128)(2,1)S(1)}, u32[]{:S(2)}, u32[]{:S(2)}) collective-permute-start(bf16[2,4,24,1536]{3,2,1,0:T(8,128)(2,1)S(1)} %dynamic-slice_bitcast_fusion.6), channel_id=1, source_target_pairs={{0,16},{4,20},{8,24},{12,28},{16,0},{20,4},{24,8},{28,12},{1,17},{... | collective-permute-start | bytes 1769480 | tf_op jit(solution)/shard_map/ppermute | solution.py:206
  570.2 16.9 %collective-permute-start.32 = (bf16[4,96,384]{2,1,0:T(8,128)(2,1)S(1)}, bf16[4,96,384]{2,1,0:T(8,128)(2,1)S(1)}, u32[]{:S(2)}, u32[]{:S(2)}) collective-permute-start(bf16[4,96,384]{2,1,0:T(8,128)(2,1)S(1)} %dynamic-slice_bitcast_fusion.11), channel_id=1, source_target_pairs={{0,16},{4,20},{8,24},{12,28},{16,0},{20,4},{24,8},{28,12},{1,17},{... | collective-permute-start | bytes 884744 | tf_op jit(solution)/shard_map/ppermute | solution.py:206
  571.1 16.1 %collective-permute-start.34 = (bf16[4,96,384]{2,1,0:T(8,128)(2,1)S(1)}, bf16[4,96,384]{2,1,0:T(8,128)(2,1)S(1)}, u32[]{:S(2)}, u32[]{:S(2)}) collective-permute-start(bf16[4,96,384]{2,1,0:T(8,128)(2,1)S(1)} %dynamic-slice_bitcast_fusion.10), channel_id=1, source_target_pairs={{0,8},{4,12},{8,0},{12,4},{16,24},{20,28},{24,16},{28,20},{1,9},{5... | collective-permute-start | bytes 884744 | tf_op jit(solution)/shard_map/ppermute | solution.py:206
  582.8 9.0 %collective-permute-start.24 = (bf16[4,24,1536]{2,1,0:T(8,128)(2,1)S(1)}, bf16[4,24,1536]{2,1,0:T(8,128)(2,1)S(1)}, u32[]{:S(2)}, u32[]{:S(2)}) collective-permute-start(bf16[4,24,1536]{2,1,0:T(8,128)(2,1)S(1)} %dynamic-slice_bitcast_fusion.13), channel_id=1, source_target_pairs={{0,16},{4,20},{8,24},{12,28},{16,0},{20,4},{24,8},{28,12},{1,17},{... | collective-permute-start | bytes 884744 | tf_op jit(solution)/shard_map/ppermute | solution.py:206
  583.3 8.6 %collective-permute-start.26 = (bf16[4,24,1536]{2,1,0:T(8,128)(2,1)S(1)}, bf16[4,24,1536]{2,1,0:T(8,128)(2,1)S(1)}, u32[]{:S(2)}, u32[]{:S(2)}) collective-permute-start(bf16[4,24,1536]{2,1,0:T(8,128)(2,1)S(1)} %dynamic-slice_bitcast_fusion.12), channel_id=1, source_target_pairs={{0,8},{4,12},{8,0},{12,4},{16,24},{20,28},{24,16},{28,20},{1,9},{5... | collective-permute-start | bytes 884744 | tf_op jit(solution)/shard_map/ppermute | solution.py:206
  587.3 7.8 %collective-permute-start.35 = (bf16[96,768]{1,0:T(8,128)(2,1)S(1)}, bf16[96,768]{1,0:T(8,128)(2,1)S(1)}, u32[]{:S(2)}, u32[]{:S(2)}) collective-permute-start(bf16[96,768]{1,0:T(8,128)(2,1)S(1)} %get-tuple-element.54), channel_id=1, source_target_pairs={{0,1},{1,0},{2,3},{3,2},{4,5},{5,4},{6,7},{7,6},{8,9},{9,8},{10,11... | collective-permute-start | bytes 442376 | tf_op jit(solution)/shard_map/ppermute | solution.py:233
  587.4 16.8 %collective-permute-start.36 = (bf16[96,768]{1,0:T(8,128)(2,1)S(1)}, bf16[96,768]{1,0:T(8,128)(2,1)S(1)}, u32[]{:S(2)}, u32[]{:S(2)}) collective-permute-start(bf16[96,768]{1,0:T(8,128)(2,1)S(1)} %get-tuple-element.55), channel_id=1, source_target_pairs={{0,2},{1,3},{2,0},{3,1},{4,6},{5,7},{6,4},{7,5},{8,10},{9,11},{10,... | collective-permute-start | bytes 442376 | tf_op jit(solution)/shard_map/ppermute | solution.py:233
  590.4 13.8 %collective-permute-start.37 = (bf16[96,768]{1,0:T(8,128)(2,1)S(1)}, bf16[96,768]{1,0:T(8,128)(2,1)S(1)}, u32[]{:S(2)}, u32[]{:S(2)}) collective-permute-start(bf16[96,768]{1,0:T(8,128)(2,1)S(1)} %get-tuple-element.56), channel_id=1, source_target_pairs={{0,3},{1,2},{2,1},{3,0},{4,7},{5,6},{6,5},{7,4},{8,11},{9,10},{10,... | collective-permute-start | bytes 442376 | tf_op jit(solution)/shard_map/ppermute | solution.py:233
  592.0 13.0 %collective-permute-start.27 = (bf16[24,3072]{1,0:T(8,128)(2,1)S(1)}, bf16[24,3072]{1,0:T(8,128)(2,1)S(1)}, u32[]{:S(2)}, u32[]{:S(2)}) collective-permute-start(bf16[24,3072]{1,0:T(8,128)(2,1)S(1)} %get-tuple-element.57), channel_id=1, source_target_pairs={{0,1},{1,0},{2,3},{3,2},{4,5},{5,4},{6,7},{7,6},{8,9},{9,8},{10,11... | collective-permute-start | bytes 442376 | tf_op jit(solution)/shard_map/ppermute | solution.py:233
  592.1 15.3 %collective-permute-start.28 = (bf16[24,3072]{1,0:T(8,128)(2,1)S(1)}, bf16[24,3072]{1,0:T(8,128)(2,1)S(1)}, u32[]{:S(2)}, u32[]{:S(2)}) collective-permute-start(bf16[24,3072]{1,0:T(8,128)(2,1)S(1)} %get-tuple-element.58), channel_id=1, source_target_pairs={{0,2},{1,3},{2,0},{3,1},{4,6},{5,7},{6,4},{7,5},{8,10},{9,11},{10,... | collective-permute-start | bytes 442376 | tf_op jit(solution)/shard_map/ppermute | solution.py:233
  595.1 12.3 %collective-permute-start.29 = (bf16[24,3072]{1,0:T(8,128)(2,1)S(1)}, bf16[24,3072]{1,0:T(8,128)(2,1)S(1)}, u32[]{:S(2)}, u32[]{:S(2)}) collective-permute-start(bf16[24,3072]{1,0:T(8,128)(2,1)S(1)} %get-tuple-element.59), channel_id=1, source_target_pairs={{0,3},{1,2},{2,1},{3,0},{4,7},{5,6},{6,5},{7,4},{8,11},{9,10},{10,... | collective-permute-start | bytes 442376 | tf_op jit(solution)/shard_map/ppermute | solution.py:233
  (54 other events, 181.8 us)
